TPU v7x, 32 devices: a whole 2x2x4 slice. The times are simulated.
32 devices in a mesh: space: 4 (over y, x), orb: 8 (over z, core).
Axes of the slice: x: 2, y: 2, z: 4, core: 2. Of those that a mesh axis runs over, the one named last changes fastest.
Arguments:
- orbitals: float32 [16, 16, 32, 1024], P('space', None, None, 'orb'), may hold values from -6 to 6
- potential: float32 [16, 16, 32], P('space'), may hold values from 0 to 2
Outputs:
- updated: float32 [16, 16, 32, 1024], P('space', None, None, 'orb')
All inputs are finite; a program needn't handle non-finite values.
Results may differ from a plain program's by a relative error of at most 0.00007.
Values sent between devices are 32-bit elements; how exact they have to be, the bound alone decides.
A program may use at most 64 MiB of HBM per device.

v0:
```python
import functools

import jax
import jax.numpy as jnp
from jax import lax
from jax.experimental import pallas as pl
from jax.experimental.pallas import tpu as pltpu
from jax.sharding import PartitionSpec as P

PANEL = 512
DEGREE = 4

STENCIL = (-205.0 / 72.0, 8.0 / 5.0, -1.0 / 5.0, 8.0 / 315.0, -1.0 / 560.0)
SHIFT_MID = 7.25
HALF_WIDTH = 4.75
LANES = 128
REACH = 4
MESH = pl.DeviceIdType.MESH
HIGHEST = lax.Precision.HIGHEST


def dot(a, b, dims):
    return lax.dot_general(
        a, b, ((dims[:1], dims[1:]), ((), ())), precision=HIGHEST, preferred_element_type=jnp.float32
    )


def regroup(load, store, count, rows):
    width = LANES // count
    step = min(rows, max(8, 128 // count))
    group = lax.broadcasted_iota(jnp.int32, (step, LANES), 1) // width

    def body(block, carry):
        here = pl.ds(pl.multiple_of(block * step, step), step)
        parts = [load(r, here) for r in range(count)]
        for j in range(count):
            out = None
            for r in range(count):
                turn = ((r - j) * width) % LANES
                piece = pltpu.roll(parts[r], turn, 1) if turn else parts[r]
                out = piece if out is None else jnp.where(group == r, piece, out)
            store(j, here, out)
        return carry

    lax.fori_loop(0, rows // step, body, 0)


def exchange(slots, here, send_sem, recv_sem, send, land):
    copies = []
    for hop in range(1, slots):
        there = lax.rem(here + hop, slots)
        copy = pltpu.make_async_remote_copy(
            src_ref=send(there),
            dst_ref=land.at[here],
            send_sem=send_sem.at[hop],
            recv_sem=recv_sem.at[hop],
            device_id={"space": there},
            device_id_type=MESH,
        )
        copy.start()
        copies.append(copy)
    return copies


def wait_exchange(slots, here, send_sem, recv_sem, send, land):
    for hop in range(1, slots):
        there = lax.rem(here + hop, slots)
        source = lax.rem(here + slots - hop, slots)
        pltpu.make_async_remote_copy(
            src_ref=send(there),
            dst_ref=land.at[source],
            send_sem=send_sem.at[hop],
            recv_sem=recv_sem.at[hop],
            device_id={"space": there},
            device_id_type=MESH,
        ).wait()


def gather_orb(count, me, buf, send_sem, recv_sem, side_send, side_recv, arrived=lambda chip: None, during=None):
    chips = count // 2
    chip, core = me // 2, lax.rem(me, 2)
    partner = chip * 2 + (1 - core)

    def along(origin, to, way, step):
        slot = buf.at[origin * 2 + core]
        return pltpu.make_async_remote_copy(
            src_ref=slot,
            dst_ref=slot,
            send_sem=send_sem.at[way, step],
            recv_sem=recv_sem.at[way, step],
            device_id={"orb": to * 2 + core},
            device_id_type=MESH,
        )

    def across(origin, side, index):
        slot = buf.at[origin * 2 + side]
        return pltpu.make_async_remote_copy(
            src_ref=slot,
            dst_ref=slot,
            send_sem=side_send.at[index],
            recv_sem=side_recv.at[index],
            device_id={"orb": partner},
            device_id_type=MESH,
        )

    steps = chips - 1

    def finish(step):
        @pl.when(chip - 1 - step >= 0)
        def _():
            across(chip - 1 - step, 1 - core, 1 + step).wait_recv()
            arrived(chip - 1 - step)

        @pl.when(chip + 1 + step < chips)
        def _():
            across(chip + 1 + step, 1 - core, 1 + steps + step).wait_recv()
            arrived(chip + 1 + step)

    for step in range(steps):
        @pl.when((chip - step >= 0) & (chip + 1 < chips))
        def _():
            along(chip - step, chip + 1, 0, step).start()

        @pl.when((chip + step < chips) & (chip - 1 >= 0))
        def _():
            along(chip + step, chip - 1, 1, step).start()

        if step == 0:
            across(chip, core, 0).start()
            if during:
                during[0]()
        if step == (1 if during else 0):
            if during:
                during[1]()
            across(chip, 1 - core, 0).wait_recv()
            arrived(chip)
        if step:
            finish(step - 1)

        @pl.when(chip - 1 - step >= 0)
        def _():
            along(chip - 1 - step, chip, 0, step).wait_recv()
            across(chip - 1 - step, core, 1 + step).start()

        @pl.when(chip + 1 + step < chips)
        def _():
            along(chip + 1 + step, chip, 1, step).wait_recv()
            across(chip + 1 + step, core, 1 + steps + step).start()

    finish(steps - 1)
    across(chip, core, 0).wait_send()
    for step in range(steps):
        @pl.when((chip - step >= 0) & (chip + 1 < chips))
        def _():
            along(chip - step, chip + 1, 0, step).wait_send()

        @pl.when((chip + step < chips) & (chip - 1 >= 0))
        def _():
            along(chip + step, chip - 1, 1, step).wait_send()

        @pl.when(chip - 1 - step >= 0)
        def _():
            across(chip - 1 - step, core, 1 + step).wait_send()

        @pl.when(chip + 1 + step < chips)
        def _():
            across(chip + 1 + step, core, 1 + steps + step).wait_send()


def split_filter(
    slabs, shape, here, me, x_ref, pot_ref, own_ref, pack, land, pack_back, land_back, pot_land,
    wide_a, wide_b, level, gath, out_sems, pot_sems, back_sems,
):
    planes, rows_y, rows_z = shape
    points = planes * rows_y * rows_z
    slots = 2 * slabs
    width = LANES // slots
    rows = points // slots
    plane = 3 * rows
    thin = points // LANES
    step = 16
    slot = lax.broadcasted_iota(jnp.int32, (step, LANES), 1) // width

    def merge(parts):
        out = None
        for u, (value, v) in enumerate(parts):
            turn = ((u - v) * width) % LANES
            value = pltpu.roll(value, turn, 1) if turn else value
            out = value if out is None else jnp.where(slot == u, value, out)
        return out

    def over(body):
        def one(block, carry):
            body(pl.multiple_of(block * step, step))
            return carry

        lax.fori_loop(0, rows // step, one, 0)

    def half(buf, h):
        return buf.at[:, h * rows : (h + 1) * rows]

    def send(buf, landing, h, sems):
        exchange(slabs, here, *sems[h], lambda there: half(buf, h).at[there], half(landing, h))
        landing[here, h * rows : (h + 1) * rows] = buf[here, h * rows : (h + 1) * rows]

    def wait(buf, landing, h, sems):
        wait_exchange(slabs, here, *sems[h], lambda there: half(buf, h).at[there], half(landing, h))

    def pack_half(h):
        def body(at):
            parts = [x_ref[pl.ds(q * rows + at, step), :] for q in range(slots)]
            for j in range(slabs):
                pack[j, pl.ds(h * rows + at, step), :] = merge([(part, h * slabs + j) for part in parts])

        over(body)
        send(pack, land, h, out_sems)

    def put(target, p, row, value):
        odd = lax.rem(lax.broadcasted_iota(jnp.int32, value.shape, 1) // width, 2)
        size = value.shape[0]
        swapped = jnp.where(odd == 0, pltpu.roll(value, LANES - width, 1), pltpu.roll(value, width, 1))
        target[pl.ds((planes + p) * plane + rows + row, size), :] = value
        target[pl.ds((planes + p) * plane + row, size), :] = swapped
        target[pl.ds((planes + p) * plane + 2 * rows + row, size), :] = swapped
        target[pl.ds(p * plane + rows + row, size), :] = pltpu.roll(value, 2 * width, 1)
        target[pl.ds((2 * planes + p) * plane + rows + row, size), :] = pltpu.roll(value, LANES - 2 * width, 1)

    taps = [-0.5 * c / HALF_WIDTH for c in STENCIL]

    def sweep(source, target, first):
        def body(y, carry):
            for p in range(planes):
                def line(q, yy):
                    row = pl.multiple_of((planes + q) * plane + rows + yy * rows_z, rows_z)
                    return source[pl.ds(row, rows_z), :]

                row = pl.multiple_of(y * rows_z, rows_z)
                centre = line(p, y)
                total = level[pl.ds(p * rows + row, rows_z), :] * centre
                for m in range(1, REACH + 1):
                    near = line(p + m, y) + line(p - m, y) + line(p, y + m) + line(p, y - m)
                    near += pltpu.roll(centre, m, 0) + pltpu.roll(centre, rows_z - m, 0)
                    total += taps[m] * near
                if not first:
                    total = 2.0 * total - target[pl.ds((planes + p) * plane + rows + row, rows_z), :]
                put(target, p, row, total)
            return carry

        lax.fori_loop(0, rows_y // 2, body, 0)

    def filter_half(h):
        wait(pack, land, h, out_sems)

        def unpack(at):
            parts = [land[i, pl.ds(h * rows + at, step), :] for i in range(slabs)]
            for p in range(planes):
                put(wide_a, p, at, merge([(parts[u // 2], 2 * p + u % 2) for u in range(slots)]))

        over(unpack)
        sweep(wide_a, wide_b, True)
        source, target = wide_b, wide_a
        for _ in range(DEGREE - 1):
            sweep(source, target, False)
            source, target = target, source

        def body(at):
            parts = [source[pl.ds((planes + p) * plane + rows + at, step), :] for p in range(planes)]
            for i in range(slabs):
                pack_back[i, pl.ds(h * rows + at, step), :] = merge(
                    [(parts[q // 2], 2 * i + q % 2) for q in range(slots)]
                )

        over(body)
        send(pack_back, land_back, h, back_sems)

    pack_half(0)
    pack_half(1)
    pot_land[here] = pot_ref[...]
    wait_exchange(slabs, here, *pot_sems, lambda there: pot_ref, pot_land)
    lane_slot = lax.broadcasted_iota(jnp.int32, (thin, LANES), 1) // width
    fields = [pot_land[s] for s in range(slabs)]
    pieces = rows // thin
    for p in range(planes):
        for e in range(pieces):
            value = None
            for u in range(slots):
                l = (2 * p + u % 2) * pieces + e
                spread = jnp.broadcast_to(fields[u // 2][:, l : l + 1], (thin, LANES))
                value = spread if value is None else jnp.where(lane_slot == u, spread, value)
            level[pl.ds(p * rows + e * thin, thin), :] = (
                value - (SHIFT_MID + 1.5 * STENCIL[0])
            ) * (1.0 / HALF_WIDTH)

    filter_half(0)
    wait(pack_back, land_back, 0, back_sems)

    def fold_own(at):
        parts = [land_back[j, pl.ds(at, step), :] for j in range(slabs)]
        for k in range(slabs):
            gath[me, pl.ds(k * rows + at, step), :] = merge(
                [(parts[u % slabs], (u // slabs) * slabs + k) for u in range(slots)]
            )

    over(fold_own)

    def finish():
        wait(pack_back, land_back, 1, back_sems)

        def body(at):
            parts = [
                land_back[u % slabs, pl.ds((u // slabs) * rows + at, step), :] for u in range(slots)
            ]
            for q in range(slots):
                own_ref[pl.ds(q * rows + at, step), :] = merge([(part, q) for part in parts])

        over(body)

    return (lambda: filter_half(1)), finish


def filter_kernel(
    slabs, orbs, shape, split,
    x_ref, pot_ref, own_ref, panel_ref, gram_ref, cross_ref,
    pack, land, pack_back, land_back, pot_land, wide_a, wide_b, level, gath, part, part_land, rows_land,
    a_send, a_recv, p_send, p_recv, b_send, b_recv, c_send, c_recv, d_send, d_recv, e_send, e_recv, f_send, f_recv,
    g_send, g_recv, gs_send, gs_recv, h_send, h_recv, hs_send, hs_recv,
):
    planes, rows_y, rows_z = shape
    points = planes * rows_y * rows_z
    here, me = lax.axis_index("space"), lax.axis_index("orb")
    chunk = points // slabs
    width = LANES // slabs

    barrier = pltpu.get_barrier_semaphore()
    for hop in range(1, slabs):
        pl.semaphore_signal(
            barrier, inc=1, device_id={"space": lax.rem(here + hop, slabs)}, device_id_type=MESH
        )
    for hop in range(1, orbs):
        pl.semaphore_signal(
            barrier, inc=1, device_id={"orb": lax.rem(me + hop, orbs)}, device_id_type=MESH
        )
    pl.semaphore_wait(barrier, slabs - 1 + orbs - 1)

    exchange(slabs, here, p_send, p_recv, lambda there: pot_ref, pot_land)

    panel_dev = PANEL // orbs
    folds = LANES // panel_dev
    fold = points // folds
    during = None
    if split:
        during = split_filter(
            slabs, shape, here, me, x_ref, pot_ref, own_ref, pack, land, pack_back, land_back, pot_land,
            wide_a, wide_b, level, gath,
            ((a_send, a_recv), (e_send, e_recv)), (p_send, p_recv), ((b_send, b_recv), (f_send, f_recv)),
        )
    else:
        def store_pack(j, at, value):
            pack[j, at, :] = value

        regroup(lambda r, at: x_ref[pl.ds(r * chunk + at.start, at.size), :], store_pack, slabs, chunk)
        exchange(slabs, here, a_send, a_recv, lambda there: pack.at[there], land)
        land[here] = pack[here]
        pot_land[here] = pot_ref[...]
        wait_exchange(slabs, here, p_send, p_recv, lambda there: pot_ref, pot_land)

        thin = points // LANES
        lane_group = lax.broadcasted_iota(jnp.int32, (thin, LANES), 1) // width
        fields = [pot_land[s] for s in range(slabs)]
        for l in range(LANES):
            value = None
            for s in range(slabs):
                spread = jnp.broadcast_to(fields[s][:, l : l + 1], (thin, LANES))
                value = spread if value is None else jnp.where(lane_group == s, spread, value)
            level[pl.ds(l * thin, thin), :] = (value - (SHIFT_MID + 1.5 * STENCIL[0])) * (1.0 / HALF_WIDTH)

        wait_exchange(slabs, here, a_send, a_recv, lambda there: pack.at[there], land)

        def put(target, row, value):
            target[pl.ds(points + row, value.shape[0]), :] = value
            target[pl.ds(row, value.shape[0]), :] = pltpu.roll(value, width, 1)
            target[pl.ds(2 * points + row, value.shape[0]), :] = pltpu.roll(value, LANES - width, 1)

        regroup(
            lambda r, at: land[r, at, :],
            lambda j, at, value: put(wide_a, j * chunk + at.start, value),
            slabs, chunk,
        )

        plane = rows_y * rows_z
        taps = [-0.5 * c / HALF_WIDTH for c in STENCIL]

        def sweep(source, target, first):
            def body(y, carry):
                for p in range(planes):
                    def line(q, yy):
                        return source[pl.ds(pl.multiple_of(points + q * plane + yy * rows_z, rows_z), rows_z), :]

                    row = pl.multiple_of(p * plane + y * rows_z, rows_z)
                    centre = line(p, y)
                    total = level[pl.ds(row, rows_z), :] * centre
                    for m in range(1, REACH + 1):
                        near = line(p + m, y) + line(p - m, y)
                        near += line(p, lax.rem(y + m, rows_y)) + line(p, lax.rem(y + rows_y - m, rows_y))
                        near += pltpu.roll(centre, m, 0) + pltpu.roll(centre, rows_z - m, 0)
                        total += taps[m] * near
                    if not first:
                        before = target[pl.ds(pl.multiple_of(points + row, rows_z), rows_z), :]
                        total = 2.0 * total - before
                    put(target, row, total)
                return carry

            lax.fori_loop(0, rows_y, body, 0)

        sweep(wide_a, wide_b, True)
        source, target = wide_b, wide_a
        for _ in range(DEGREE - 1):
            sweep(source, target, False)
            source, target = target, source

        def store_back(j, at, value):
            pack_back[j, at, :] = value

        regroup(
            lambda r, at: source[pl.ds(points + r * chunk + at.start, at.size), :], store_back, slabs, chunk
        )
        exchange(slabs, here, b_send, b_recv, lambda there: pack_back.at[there], land_back)
        land_back[here] = pack_back[here]
        wait_exchange(slabs, here, b_send, b_recv, lambda there: pack_back.at[there], land_back)

        def store_own(j, at, value):
            own_ref[pl.ds(j * chunk + at.start, at.size), :] = value

        regroup(lambda r, at: land_back[r, at, :], store_own, slabs, chunk)

        step = min(fold, 32)
        fold_group = lax.broadcasted_iota(jnp.int32, (step, LANES), 1) // panel_dev

        def folded(block, carry):
            at = pl.multiple_of(block * step, step)
            out = None
            for r in range(folds):
                piece = own_ref[pl.ds(r * fold + at, step), :]
                piece = pltpu.roll(piece, r * panel_dev, 1) if r else piece
                out = piece if out is None else jnp.where(fold_group == r, piece, out)
            gath[me, pl.ds(at, step), :] = out
            return carry

        lax.fori_loop(0, fold // step, folded, 0)

    block = 512

    def take(tile):
        lanes = pl.ds(pl.multiple_of(tile * LANES, LANES), LANES)

        def store_panel(j, at, value):
            panel_ref[pl.ds(j * fold + at.start, at.size), lanes] = value

        regroup(lambda r, at: gath[tile * folds + r, at, :], store_panel, folds, fold)

        def product(k, total):
            at = pl.ds(pl.multiple_of(k * block, block), block)
            return total + dot(own_ref[at, :], panel_ref[at, lanes], (0, 0))

        part[:, lanes] = lax.fori_loop(
            0, points // block, product, jnp.zeros((LANES, LANES), jnp.float32)
        )

    if folds == 2:
        gather_orb(orbs, me, gath, g_send, g_recv, gs_send, gs_recv, take, during)
    else:
        gather_orb(orbs, me, gath, g_send, g_recv, gs_send, gs_recv)

        def each(tile, carry):
            take(tile)
            return carry

        lax.fori_loop(0, PANEL // LANES, each, 0)

    top, rest = part.at[:panel_dev], part.at[panel_dev:]
    top_land, rest_land = part_land.at[:, :panel_dev], part_land.at[:, panel_dev:]
    exchange(slabs, here, c_send, c_recv, lambda there: top, top_land)
    exchange(slabs, here, d_send, d_recv, lambda there: rest, rest_land)
    part_land[here] = part[...]
    points_all = points * slabs

    def summed(view):
        total = view[0]
        for s in range(1, slabs):
            total += view[s]
        return total / points_all

    wait_exchange(slabs, here, c_send, c_recv, lambda there: top, top_land)
    rows_land[me] = summed(top_land)
    gather_orb(orbs, me, rows_land, h_send, h_recv, hs_send, hs_recv)
    wait_exchange(slabs, here, d_send, d_recv, lambda there: rest, rest_land)
    cross_ref[:panel_dev, :] = jnp.zeros((panel_dev, PANEL), jnp.float32)
    cross_ref[panel_dev:, :] = summed(rest_land)
    for o in range(orbs):
        gram_ref[o * panel_dev : (o + 1) * panel_dev, :] = rows_land[o]


def block_inverse(a):
    n = LANES
    tiles = n // 8
    rows = lax.broadcasted_iota(jnp.int32, (8, n), 0)
    cols = lax.broadcasted_iota(jnp.int32, (8, n), 1)
    work = [a[8 * t : 8 * t + 8] for t in range(tiles)]
    unit = [jnp.where(rows + 8 * t == cols, 1.0, 0.0).astype(jnp.float32) for t in range(tiles)]
    for t0 in range(tiles):
        base = 8 * t0
        columns = [jnp.broadcast_to(work[t0][:, base + k : base + k + 1], (8, n)) for k in range(8)]
        small = {
            (i, k): jnp.broadcast_to(columns[k][i : i + 1], (8, n)) for i in range(8) for k in range(i + 1)
        }
        lower, scales = {}, []
        for j in range(8):
            scales.append(1.0 / small[j, j])
            for i in range(j + 1, 8):
                lower[i, j] = small[i, j] * scales[j]
            for i in range(j + 1, 8):
                for k in range(j + 1, i + 1):
                    small[i, k] = small[i, k] - lower[i, j] * small[k, j]
        turned = {}
        for j in range(8):
            for i in range(j + 1, 8):
                value = lower[i, j]
                for k in range(j + 1, i):
                    value = value + lower[i, k] * turned[k, j]
                turned[i, j] = -value
        a_row, u_row = work[t0], unit[t0]
        a_new, u_new = a_row, u_row
        for k in range(7):
            weight = jnp.zeros((8, n), jnp.float32)
            for i in range(k + 1, 8):
                weight = jnp.where(rows == i, turned[i, k], weight)
            a_new = a_new + weight * jnp.broadcast_to(a_row[k : k + 1], (8, n))
            u_new = u_new + weight * jnp.broadcast_to(u_row[k : k + 1], (8, n))
        work[t0], unit[t0] = a_new, u_new
        if t0 == tiles - 1:
            break
        a_out = u_out = None
        for i in range(8):
            weight = jnp.where(rows == i, scales[i], 0.0)
            for k in range(i):
                weight = jnp.where(rows == k, turned[i, k] * scales[i], weight)
            a_term = weight * jnp.broadcast_to(a_new[i : i + 1], (8, n))
            u_term = weight * jnp.broadcast_to(u_new[i : i + 1], (8, n))
            a_out = a_term if a_out is None else a_out + a_term
            u_out = u_term if u_out is None else u_out + u_term
        a_rows = [jnp.broadcast_to(a_out[k : k + 1], (8, n)) for k in range(8)]
        u_rows = [jnp.broadcast_to(u_out[k : k + 1], (8, n)) for k in range(8)]
        for t in range(t0 + 1, tiles):
            before = work[t]
            for k in range(8):
                column = jnp.broadcast_to(before[:, base + k : base + k + 1], (8, n))
                work[t] = work[t] - column * a_rows[k]
                unit[t] = unit[t] - column * u_rows[k]
    out = []
    for t in range(tiles):
        pivots = jnp.sum(jnp.where(rows + 8 * t == cols, work[t], 0.0), axis=1, keepdims=True)
        out.append(unit[t] * (1.0 / jnp.sqrt(pivots)))
    return jnp.concatenate(out, axis=0)


def solve_kernel(orbs, own_ref, panel_ref, gram_ref, cross_ref, out_ref, work, inverse, weights):
    panel_dev = PANEL // orbs
    me = lax.axis_index("orb")
    n = LANES
    blocks = PANEL // n
    work[...] = gram_ref[...]
    inverse[...] = jnp.zeros_like(inverse)

    def factor(b, carry):
        at = pl.multiple_of(b * n, n)
        diag = block_inverse(work[pl.ds(at, n), pl.ds(at, n)])
        inverse[pl.ds(at, n), pl.ds(at, n)] = diag
        for i in range(1, blocks):
            @pl.when(i > b)
            def _():
                work[i * n : (i + 1) * n, pl.ds(at, n)] = dot(
                    work[i * n : (i + 1) * n, pl.ds(at, n)], diag, (1, 1)
                )
        for i in range(1, blocks):
            @pl.when(i > b)
            def _():
                left = work[i * n : (i + 1) * n, pl.ds(at, n)]
                for k in range(1, i + 1):
                    @pl.when(k > b)
                    def _():
                        right = work[k * n : (k + 1) * n, pl.ds(at, n)]
                        work[i * n : (i + 1) * n, k * n : (k + 1) * n] -= dot(left, right, (1, 1))
        return carry

    lax.fori_loop(0, blocks, factor, 0)
    for i in range(1, blocks):
        span = i * n
        inner = dot(work[i * n : (i + 1) * n, :span], inverse[:span, :span], (1, 0))
        inverse[i * n : (i + 1) * n, :span] = -dot(
            inverse[i * n : (i + 1) * n, i * n : (i + 1) * n], inner, (1, 0)
        )

    middle = dot(cross_ref[...], inverse[...], (1, 1))
    weights[...] = -dot(middle, inverse[...], (1, 0))
    weights[:panel_dev, :] = inverse[pl.ds(pl.multiple_of(me * panel_dev, panel_dev), panel_dev), :]
    points = own_ref.shape[0]
    block = 256
    lanes = lax.broadcasted_iota(jnp.int32, (block, LANES), 1)

    def final(k, carry):
        at = pl.ds(pl.multiple_of(k * block, block), block)
        kept = jnp.where(lanes < panel_dev, 0.0, own_ref[at, :])
        out_ref[at, :] = kept + dot(panel_ref[at, :], weights[...], (1, 1))
        return carry

    lax.fori_loop(0, points // block, final, 0)


def per_device(slabs, orbs, orbitals, potential):
    planes, rows_y, rows_z, columns = orbitals.shape
    points = planes * rows_y * rows_z
    panel_dev = PANEL // orbs
    folds = LANES // panel_dev
    thin = points // LANES
    f32 = jnp.float32
    vmem = pl.BlockSpec(memory_space=pltpu.VMEM)
    dma = pltpu.SemaphoreType.DMA
    steps = max(orbs // 2 - 1, 1)
    split = folds == 2 and planes == slabs and rows_y // 2 >= REACH and steps >= 2
    flat = orbitals.reshape(points, columns)
    own, panel, gram, cross = pl.pallas_call(
        functools.partial(filter_kernel, slabs, orbs, (planes, rows_y, rows_z), split),
        out_shape=[
            jax.ShapeDtypeStruct((points, LANES), f32),
            jax.ShapeDtypeStruct((points, PANEL), f32),
            jax.ShapeDtypeStruct((PANEL, PANEL), f32),
            jax.ShapeDtypeStruct((LANES, PANEL), f32),
        ],
        in_specs=[vmem] * 2,
        out_specs=[vmem] * 4,
        scratch_shapes=[pltpu.VMEM((slabs, points // slabs, LANES), f32)] * 4
        + [
            pltpu.VMEM((slabs, thin, LANES), f32),
            pltpu.VMEM(((9 if split else 6) * points // 2, LANES), f32),
            pltpu.VMEM(((9 if split else 6) * points // 2, LANES), f32),
            pltpu.VMEM((points, LANES), f32),
            pltpu.VMEM((orbs, points // folds, LANES), f32),
            pltpu.VMEM((LANES, PANEL), f32),
            pltpu.VMEM((slabs, LANES, PANEL), f32),
            pltpu.VMEM((orbs, panel_dev, PANEL), f32),
        ]
        + [dma((slabs,))] * 14
        + [dma((2, steps))] * 2 + [dma((2 * steps + 1,))] * 2
        + [dma((2, steps))] * 2 + [dma((2 * steps + 1,))] * 2,
        compiler_params=pltpu.CompilerParams(
            collective_id=0, has_side_effects=True, vmem_limit_bytes=32 << 20
        ),
    )(flat, potential.reshape(LANES, thin).T)
    out = pl.pallas_call(
        functools.partial(solve_kernel, orbs),
        out_shape=jax.ShapeDtypeStruct((points, LANES), f32),
        in_specs=[vmem] * 4,
        out_specs=vmem,
        scratch_shapes=[
            pltpu.VMEM((PANEL, PANEL), f32),
            pltpu.VMEM((PANEL, PANEL), f32),
            pltpu.VMEM((LANES, PANEL), f32),
        ],
        compiler_params=pltpu.CompilerParams(vmem_limit_bytes=32 << 20),
    )(own, panel, gram, cross)
    return out.reshape(planes, rows_y, rows_z, columns)


def solution(mesh):
    placed = (P("space", None, None, "orb"), P("space", None, None))
    return jax.shard_map(
        functools.partial(per_device, mesh.shape["space"], mesh.shape["orb"]),
        mesh=mesh,
        in_specs=placed,
        out_specs=P("space", None, None, "orb"),
        check_vma=False,
    )
```

profile of v0, /device:TPU:0, one launch (start us, length us, event | category | flops | bytes accessed | tf_op | source)
XLA Modules:
  0.0 138.6 jit_solution(16739522170605738368)
XLA Ops:
  0.0 0.8 reshape.10
  0.8 0.1 copy.3
  0.9 0.0 copy-start
  0.9 1.2 copy-done
  2.1 104.2 %shard_map.28 = (f32[2048,128]{1,0:T(8,128)S(1)}, f32[2048,512]{1,0:T(8,128)S(1)}, f32[512,512]{1,0:T(8,128)S(1)}, f32[128,512]{1,0:T(8,128)S(1)}) custom-call(f32[2048,128]{1,0:T(8,128)S(1)} %bitcast.3, f32[16,128]{1,0:T(8,128)S(1)} %bitcast.4), custom_call_target="tpu_custom_call" | custom-call | tf_op jit(solution)/shard_map/pallas_call | solution.py:631
  106.3 32.3 %shard_map.29 = f32[2048,128]{1,0:T(8,128)} custom-call(f32[2048,128]{1,0:T(8,128)S(1)} %get-tuple-element.9.own_ref, f32[2048,512]{1,0:T(8,128)S(1)} %get-tuple-element.10.panel_ref, f32[512,512]{1,0:T(8,128)S(1)} %get-tuple-element.11.gram_ref, f32[128,512]{1,0:T(8,128)S(1)} %get-tuple-element.12.cross_ref), custom_call_target="tpu_custom_call" | custom-call | tf_op jit(solution)/shard_map/pallas_call | solution.py:659
Async XLA Ops:
  0.9 1.2 copy-start
where the time goes:
time: 139 us
  Pallas kernels  136 us (98%)
  local copies, waits for them, and re-layouts  2.13 us (2%)
    pallas_call x1, Pallas kernels, per_device(): pl.pallas_call(functools.partial(filter_kernel, slabs, orbs, (planes, row...  104 us
    pallas_call x1, Pallas kernels, per_device(): pl.pallas_call(functools.partial(solve_kernel, orbs), out_shape=jax.Shape...  32.3 us

commit v1 on v0

--- a/solution.py
+++ b/solution.py
@@ -616,6 +616,646 @@
     lax.fori_loop(0, points // block, final, 0)
 
 
+def pieces(x):
+    high = x.astype(jnp.bfloat16)
+    return high, (x - high.astype(jnp.float32)).astype(jnp.bfloat16)
+
+
+def dot_pieces(a, b, dims):
+    def one(left, right):
+        return lax.dot_general(
+            left, right, ((dims[:1], dims[1:]), ((), ())), preferred_element_type=jnp.float32
+        )
+
+    return one(a[0], b[0]) + (one(a[0], b[1]) + one(a[1], b[0]))
+
+
+def unfolded(product, rows):
+    half = LANES // 2
+    lanes = lax.broadcasted_iota(jnp.int32, (half, LANES), 1)
+    out = []
+    for r in range(rows):
+        sides = []
+        for c in range(2):
+            at = product[r * LANES : (r + 1) * LANES, c * LANES : (c + 1) * LANES]
+            sides.append(at[:half] + pltpu.roll(at[half:], half, 1))
+        out.append(jnp.where(lanes < half, sides[0], pltpu.roll(sides[1], half, 1)))
+    return out
+
+
+def link_orders():
+    up = {0: [(0, 1), (0, 0)], 1: [(1, 1), (0, 1), (1, 0), (0, 0)],
+          2: [(2, 1), (2, 0), (1, 1), (0, 1), (1, 0), (0, 0)]}
+    down = {3 - z: [(3 - o, 1 - h) for o, h in order] for z, order in up.items()}
+    return up, down
+
+
+def early_kernel(
+    slabs, orbs, shape,
+    x_ref, pot_ref, gath, rest_ref, weight_ref,
+    pack, land, pack_back, land_back, pot_land, wide_a, wide_b, level,
+    gram_part, gram_land, gram_chip, gram_all, cross_part, cross_land, cross, work, inverse,
+    a_send, a_recv, p_send, p_recv, b_send, b_recv, e_send, e_recv, f_send, f_recv,
+    along_send, along_recv, across_send, across_recv,
+    r_send, r_recv, z_send, z_recv, s_send, s_recv, t_send, t_recv, c_send, c_recv,
+):
+    planes, rows_y, rows_z = shape
+    points = planes * rows_y * rows_z
+    here, me = lax.axis_index("space"), lax.axis_index("orb")
+    chips = orbs // 2
+    chip, core = me // 2, lax.rem(me, 2)
+    partner = chip * 2 + (1 - core)
+    slots = 2 * slabs
+    width = LANES // slots
+    rows = points // slots
+    plane = 3 * rows
+    thin = points // LANES
+    fold = points // 2
+    part_rows = fold // 2
+    panel_dev = PANEL // orbs
+    points_all = points * slabs
+    step = 16
+    slot = lax.broadcasted_iota(jnp.int32, (step, LANES), 1) // width
+    out_sems, back_sems = ((a_send, a_recv), (e_send, e_recv)), ((b_send, b_recv), (f_send, f_recv))
+
+    barrier = pltpu.get_barrier_semaphore()
+    for hop in range(1, slabs):
+        pl.semaphore_signal(
+            barrier, inc=1, device_id={"space": lax.rem(here + hop, slabs)}, device_id_type=MESH
+        )
+    for hop in range(1, orbs):
+        pl.semaphore_signal(
+            barrier, inc=1, device_id={"orb": lax.rem(me + hop, orbs)}, device_id_type=MESH
+        )
+
+    def merge(parts):
+        out = None
+        for u, (value, v) in enumerate(parts):
+            turn = ((u - v) * width) % LANES
+            value = pltpu.roll(value, turn, 1) if turn else value
+            out = value if out is None else jnp.where(slot == u, value, out)
+        return out
+
+    def over(body):
+        def one(block, carry):
+            body(pl.multiple_of(block * step, step))
+            return carry
+
+        lax.fori_loop(0, rows // step, one, 0)
+
+    def half(buf, h):
+        return buf.at[:, h * rows : (h + 1) * rows]
+
+    def send(buf, landing, h, sems):
+        exchange(slabs, here, *sems[h], lambda there: half(buf, h).at[there], half(landing, h))
+        landing[here, h * rows : (h + 1) * rows] = buf[here, h * rows : (h + 1) * rows]
+
+    def wait(buf, landing, h, sems):
+        wait_exchange(slabs, here, *sems[h], lambda there: half(buf, h).at[there], half(landing, h))
+
+    def pack_half(h):
+        def body(at):
+            parts = [x_ref[pl.ds(q * rows + at, step), :] for q in range(slots)]
+            for j in range(slabs):
+                pack[j, pl.ds(h * rows + at, step), :] = merge([(part, h * slabs + j) for part in parts])
+
+        over(body)
+
+    def put(target, p, row, value):
+        odd = lax.rem(lax.broadcasted_iota(jnp.int32, value.shape, 1) // width, 2)
+        size = value.shape[0]
+        swapped = jnp.where(odd == 0, pltpu.roll(value, LANES - width, 1), pltpu.roll(value, width, 1))
+        target[pl.ds((planes + p) * plane + rows + row, size), :] = value
+        target[pl.ds((planes + p) * plane + row, size), :] = swapped
+        target[pl.ds((planes + p) * plane + 2 * rows + row, size), :] = swapped
+        target[pl.ds(p * plane + rows + row, size), :] = pltpu.roll(value, 2 * width, 1)
+        target[pl.ds((2 * planes + p) * plane + rows + row, size), :] = pltpu.roll(value, LANES - 2 * width, 1)
+
+    taps = [-0.5 * c / HALF_WIDTH for c in STENCIL]
+
+    def sweep(source, target, first):
+        def body(y, carry):
+            for p in range(planes):
+                def line(q, yy):
+                    row = pl.multiple_of((planes + q) * plane + rows + yy * rows_z, rows_z)
+                    return source[pl.ds(row, rows_z), :]
+
+                row = pl.multiple_of(y * rows_z, rows_z)
+                centre = line(p, y)
+                total = level[pl.ds(p * rows + row, rows_z), :] * centre
+                for m in range(1, REACH + 1):
+                    near = line(p + m, y) + line(p - m, y) + line(p, y + m) + line(p, y - m)
+                    near += pltpu.roll(centre, m, 0) + pltpu.roll(centre, rows_z - m, 0)
+                    total += taps[m] * near
+                if not first:
+                    total = 2.0 * total - target[pl.ds((planes + p) * plane + rows + row, rows_z), :]
+                put(target, p, row, total)
+            return carry
+
+        lax.fori_loop(0, rows_y // 2, body, 0)
+
+    def filter_half(h, during=None):
+        with jax.named_scope("wait_a"):
+            wait(pack, land, h, out_sems)
+
+        def unpack(at):
+            parts = [land[i, pl.ds(h * rows + at, step), :] for i in range(slabs)]
+            for p in range(planes):
+                put(wide_a, p, at, merge([(parts[u // 2], 2 * p + u % 2) for u in range(slots)]))
+
+        with jax.named_scope("unpack"):
+            over(unpack)
+        with jax.named_scope("sweep"):
+            sweep(wide_a, wide_b, True)
+            source, target = wide_b, wide_a
+            for order in range(DEGREE - 1):
+                if during and order == DEGREE - 2:
+                    during()
+                sweep(source, target, False)
+                source, target = target, source
+
+        def body(at):
+            parts = [source[pl.ds((planes + p) * plane + rows + at, step), :] for p in range(planes)]
+            for i in range(slabs):
+                pack_back[i, pl.ds(h * rows + at, step), :] = merge(
+                    [(parts[q // 2], 2 * i + q % 2) for q in range(slots)]
+                )
+
+        with jax.named_scope("pack_b"):
+            over(body)
+            send(pack_back, land_back, h, back_sems)
+
+    def fold_half(h, store):
+        with jax.named_scope("wait_b"):
+            wait(pack_back, land_back, h, back_sems)
+
+        def body(at):
+            parts = [land_back[j, pl.ds(h * rows + at, step), :] for j in range(slabs)]
+            for k in range(slabs):
+                store(
+                    pl.ds(k * rows + at, step),
+                    merge([(parts[u % slabs], (u // slabs) * slabs + k) for u in range(slots)]),
+                )
+
+        with jax.named_scope("fold"):
+            over(body)
+
+    with jax.named_scope("pack"):
+        pack_half(0)
+    with jax.named_scope("barrier"):
+        pl.semaphore_wait(barrier, slabs - 1 + orbs - 1)
+    exchange(slabs, here, p_send, p_recv, lambda there: pot_ref, pot_land)
+    send(pack, land, 0, out_sems)
+    with jax.named_scope("pack"):
+        pack_half(1)
+    send(pack, land, 1, out_sems)
+    pot_land[here] = pot_ref[...]
+    with jax.named_scope("level"):
+        wait_exchange(slabs, here, p_send, p_recv, lambda there: pot_ref, pot_land)
+        lane_slot = lax.broadcasted_iota(jnp.int32, (thin, LANES), 1) // width
+        fields = [pot_land[s] for s in range(slabs)]
+        for p in range(planes):
+            for e in range(rows // thin):
+                value = None
+                for u in range(slots):
+                    l = (2 * p + u % 2) * (rows // thin) + e
+                    spread = jnp.broadcast_to(fields[u // 2][:, l : l + 1], (thin, LANES))
+                    value = spread if value is None else jnp.where(lane_slot == u, spread, value)
+                level[pl.ds(p * rows + e * thin, thin), :] = (
+                    value - (SHIFT_MID + 1.5 * STENCIL[0])
+                ) * (1.0 / HALF_WIDTH)
+
+    up, down = link_orders()
+
+    def along(origin, h, way):
+        view = gath.at[origin * 2 + core, h * part_rows : (h + 1) * part_rows]
+        return pltpu.make_async_remote_copy(
+            src_ref=view,
+            dst_ref=view,
+            send_sem=along_send.at[way, origin * 2 + h],
+            recv_sem=along_recv.at[way, origin * 2 + h],
+            device_id={"orb": (chip + 1 - 2 * way) * 2 + core},
+            device_id_type=MESH,
+        )
+
+    def across(origin, h, side):
+        view = gath.at[origin * 2 + side, h * part_rows : (h + 1) * part_rows]
+        return pltpu.make_async_remote_copy(
+            src_ref=view,
+            dst_ref=view,
+            send_sem=across_send.at[origin * 2 + h],
+            recv_sem=across_recv.at[origin * 2 + h],
+            device_id={"orb": partner},
+            device_id_type=MESH,
+        )
+
+    def on_chip(z, body):
+        pl.when(chip == z)(body)
+
+    def arrivals(z, t):
+        found = []
+        for way, orders in ((0, up), (1, down)):
+            order = orders.get(z - 1 + 2 * way, [])
+            if t < len(order):
+                found.append((way, order[t]))
+        return found
+
+    def begin():
+        for z in range(chips):
+            def body():
+                for way, orders in ((0, up), (1, down)):
+                    if z in orders:
+                        for item in orders[z]:
+                            if item[0] != z:
+                                break
+                            along(*item, way).start()
+                for h in range(2):
+                    across(z, h, core).start()
+
+            on_chip(z, body)
+
+    def receive(t):
+        with jax.named_scope("receive"):
+            for z in range(chips):
+                def body():
+                    for way, item in arrivals(z, t):
+                        along(*item, way).wait_recv()
+                        across(*item, core).start()
+
+                on_chip(z, body)
+
+    def forward(t):
+        for z in range(chips):
+            def body():
+                for way, item in arrivals(z, t):
+                    order = (up, down)[way].get(z, [])
+                    if item in order:
+                        along(*item, way).start()
+                        for later in order[order.index(item) + 1 :]:
+                            if later[0] != z:
+                                break
+                            along(*later, way).start()
+
+            on_chip(z, body)
+
+    def settle(t):
+        with jax.named_scope("settle"):
+            for z in range(chips):
+                def body():
+                    for way, item in arrivals(z, t):
+                        across(*item, 1 - core).wait_recv()
+
+                on_chip(z, body)
+
+    def settle_own():
+        for z in range(chips):
+            def body():
+                for h in range(2):
+                    across(z, h, 1 - core).wait_recv()
+
+            on_chip(z, body)
+
+    def drain():
+        for z in range(chips):
+            def body():
+                for way, orders in ((0, up), (1, down)):
+                    for item in orders.get(z, []):
+                        along(*item, way).wait_send()
+                for h in range(2):
+                    across(z, h, core).wait_send()
+                for t in range(2 * (chips - 1)):
+                    for way, item in arrivals(z, t):
+                        across(*item, core).wait_send()
+
+            on_chip(z, body)
+
+    filter_half(0)
+
+    def store_panel(at, value):
+        gath[me, at, :] = value
+
+    fold_half(0, store_panel)
+    begin()
+
+    def first():
+        receive(0)
+        forward(0)
+
+    filter_half(1, first)
+    receive(1)
+    settle_own()
+    settle(0)
+    settle(1)
+
+    tiles = chips * (chips + 1) // 2
+    share = tiles // 2
+    block = share * LANES // slabs
+    centre = (chip + 1) // 2 == 1
+
+    def block_at(s):
+        return pl.ds(pl.multiple_of(s * block, 8), block)
+
+    def pair(z, at):
+        return jnp.concatenate([gath[z * 2, at, :], gath[z * 2 + 1, at, :]], axis=1)
+
+    @pl.when(centre)
+    def _():
+        at = pl.ds(pl.multiple_of((chip - 1) * part_rows, part_rows), part_rows)
+
+        def tile(n, carry):
+            t = core * share + n
+            za = (t + 8) // 9 + (t + 6) // 9 + (t + 3) // 9
+            zb = t - za * (za + 1) // 2
+            product = dot_pieces(pieces(pair(za, at)), pieces(pair(zb, at)), (0, 0))
+            for r, value in enumerate(unfolded(product, 2)):
+                gram_part[pl.ds(pl.multiple_of(n * LANES + r * panel_dev, panel_dev), panel_dev), :] = value
+            return carry
+
+        with jax.named_scope("gram"):
+            lax.fori_loop(0, share, tile, 0)
+        exchange(slabs, here, r_send, r_recv, lambda there: gram_part.at[block_at(there)], gram_land)
+
+    def store_rest(at, value):
+        rest_ref[at, :] = value
+
+    fold_half(1, store_rest)
+
+    def spread(index, there):
+        view = gram_chip.at[index]
+        return pltpu.make_async_remote_copy(
+            src_ref=view,
+            dst_ref=view,
+            send_sem=z_send.at[there],
+            recv_sem=z_recv.at[index],
+            device_id={"orb": there * 2 + core},
+            device_id_type=MESH,
+        )
+
+    @pl.when(centre)
+    def _():
+        with jax.named_scope("wait_r"):
+            wait_exchange(slabs, here, r_send, r_recv, lambda there: gram_part.at[block_at(there)], gram_land)
+        gram_land[here] = gram_part[block_at(here), :]
+        total = gram_land[0]
+        for s in range(1, slabs):
+            total += gram_land[s]
+        gram_chip[chip - 1] = total / points_all
+
+    for z in range(1, 3):
+        def body():
+            for there in range(chips):
+                if there != z:
+                    spread(z - 1, there).start()
+
+        on_chip(z, body)
+    forward(1)
+    receive(2)
+    forward(2)
+
+    def couple(n, z):
+        rows_k = 256
+        with jax.named_scope("couple"):
+            def product(k, total):
+                at = pl.ds(pl.multiple_of(k * rows_k, rows_k), rows_k)
+                return total + dot_pieces(pieces(rest_ref[at, :]), pieces(pair(z, at)), (0, 0))
+
+            total = lax.fori_loop(
+                0, fold // rows_k, product, jnp.zeros((LANES, 2 * LANES), jnp.float32)
+            )
+            value = unfolded(total, 1)[0]
+            cross_part[n] = value
+            cross_land[n, here] = value
+        exchange(slabs, here, c_send.at[n], c_recv.at[n], lambda there: cross_part.at[n], cross_land.at[n])
+
+    lower = chip // 2
+    order = [chip, chip + 1 - 2 * lax.rem(chip, 2), 2 - lower, 3 - 3 * lower]
+    couple(0, order[0])
+
+    with jax.named_scope("wait_z"):
+        for z in range(chips):
+            def body():
+                for index in range(2):
+                    if z != index + 1:
+                        spread(index, z).wait_recv()
+                    else:
+                        for there in range(chips):
+                            if there != z:
+                                spread(index, there).wait_send()
+
+            on_chip(z, body)
+    gram_all[core, block_at(here), :] = gram_chip[0] + gram_chip[1]
+
+    def own_block(there):
+        return gram_all.at[core, block_at(here)]
+
+    def gram_side(side, s):
+        view = gram_all.at[side, block_at(s)]
+        return pltpu.make_async_remote_copy(
+            src_ref=view,
+            dst_ref=view,
+            send_sem=t_send.at[s],
+            recv_sem=t_recv.at[s],
+            device_id={"orb": partner},
+            device_id_type=MESH,
+        )
+
+    def plane_copy(hop, s, there):
+        view = gram_all.at[core, block_at(s)]
+        return pltpu.make_async_remote_copy(
+            src_ref=view,
+            dst_ref=view,
+            send_sem=s_send.at[hop],
+            recv_sem=s_recv.at[hop],
+            device_id={"space": there},
+            device_id_type=MESH,
+        )
+
+    for hop in range(1, slabs):
+        plane_copy(hop, here, lax.rem(here + hop, slabs)).start()
+    gram_side(core, here).start()
+    couple(1, order[1])
+    receive(3)
+    forward(3)
+    with jax.named_scope("wait_s"):
+        for hop in range(1, slabs):
+            source = lax.rem(here + slabs - hop, slabs)
+            plane_copy(hop, source, lax.rem(here + hop, slabs)).wait_recv()
+            gram_side(core, source).start()
+        for s in range(slabs):
+            gram_side(1 - core, s).wait_recv()
+
+    n = LANES
+    blocks = chips
+    inverse[...] = jnp.zeros_like(inverse)
+    for za in range(chips):
+        for zb in range(za + 1):
+            t = za * (za + 1) // 2 + zb
+            work[za * n : (za + 1) * n, zb * n : (zb + 1) * n] = gram_all[
+                t // share, (t % share) * n : (t % share + 1) * n, :
+            ]
+
+    def factor(b, carry):
+        at = pl.multiple_of(b * n, n)
+        with jax.named_scope("diag"):
+            diag = block_inverse(work[pl.ds(at, n), pl.ds(at, n)])
+            inverse[pl.ds(at, n), pl.ds(at, n)] = diag
+        for i in range(1, blocks):
+            @pl.when(i > b)
+            def _():
+                work[i * n : (i + 1) * n, pl.ds(at, n)] = dot(
+                    work[i * n : (i + 1) * n, pl.ds(at, n)], diag, (1, 1)
+                )
+        for i in range(1, blocks):
+            @pl.when(i > b)
+            def _():
+                left = work[i * n : (i + 1) * n, pl.ds(at, n)]
+                for k in range(1, i + 1):
+                    @pl.when(k > b)
+                    def _():
+                        right = work[k * n : (k + 1) * n, pl.ds(at, n)]
+                        work[i * n : (i + 1) * n, k * n : (k + 1) * n] -= dot(left, right, (1, 1))
+
+        @pl.when(b == 0)
+        def _():
+            receive(4)
+            forward(4)
+
+        @pl.when(b == 1)
+        def _():
+            settle(2)
+            settle(3)
+            settle(4)
+            couple(2, order[2])
+
+        @pl.when(b == 2)
+        def _():
+            receive(5)
+            settle(5)
+            couple(3, order[3])
+
+        return carry
+
+    with jax.named_scope("factor"):
+        lax.fori_loop(0, blocks, factor, 0)
+    with jax.named_scope("inverse"):
+        for i in range(1, blocks):
+            span = i * n
+            inner = dot(work[i * n : (i + 1) * n, :span], inverse[:span, :span], (1, 0))
+            inverse[i * n : (i + 1) * n, :span] = -dot(
+                inverse[i * n : (i + 1) * n, i * n : (i + 1) * n], inner, (1, 0)
+            )
+
+    with jax.named_scope("cross"):
+        for k in range(chips):
+            wait_exchange(
+                slabs, here, c_send.at[k], c_recv.at[k], lambda there: cross_part.at[k], cross_land.at[k]
+            )
+            total = cross_land[k, 0]
+            for s in range(1, slabs):
+                total += cross_land[k, s]
+            cross[:, pl.ds(pl.multiple_of(order[k] * LANES, LANES), LANES)] = total / points_all
+    with jax.named_scope("weights"):
+        middle = dot(cross[...], inverse[...], (1, 1))
+        trail = -dot(middle, inverse[...], (1, 0))
+        own = inverse[pl.ds(pl.multiple_of(me * panel_dev, panel_dev), panel_dev), :]
+        turned = jnp.concatenate([own, trail], axis=0).T
+        weight_ref[...] = jnp.zeros_like(weight_ref)
+        for o in range(orbs):
+            value = turned[o * panel_dev : (o + 1) * panel_dev]
+            weight_ref[o * LANES : o * LANES + panel_dev, :LANES] = value
+            weight_ref[o * LANES + panel_dev : (o + 1) * LANES, LANES:] = value
+    drain()
+    for hop in range(1, slabs):
+        plane_copy(hop, here, lax.rem(here + hop, slabs)).wait_send()
+    for s in range(slabs):
+        gram_side(core, s).wait_send()
+
+
+def final_kernel(gath_ref, rest_ref, weight_ref, out_ref, high, low):
+    orbs, fold, n = gath_ref.shape
+    rows = out_ref.shape[1]
+    i = pl.program_id(0)
+
+    @pl.when(i == 0)
+    def _():
+        high[...], low[...] = pieces(weight_ref[...])
+
+    at = pl.ds(pl.multiple_of(i * rows, rows), rows)
+    total = None
+    for z in range(orbs // 2):
+        k = slice(z * 2 * n, (z + 1) * 2 * n)
+        pair = jnp.concatenate([gath_ref[z * 2, at, :], gath_ref[z * 2 + 1, at, :]], axis=1)
+        value = dot_pieces(pieces(pair), (high[k, :], low[k, :]), (1, 0))
+        total = value if total is None else total + value
+    lanes = lax.broadcasted_iota(jnp.int32, (rows, n), 1)
+    kept = rest_ref[at, :]
+    for h in range(2):
+        held = kept if h else pltpu.roll(kept, n // 2, 1)
+        out_ref[h] = jnp.where(lanes < n // 2, 0.0, held) + total[:, h * n : (h + 1) * n]
+
+
+def early_device(slabs, orbs, orbitals, potential):
+    planes, rows_y, rows_z, columns = orbitals.shape
+    points = planes * rows_y * rows_z
+    panel_dev = PANEL // orbs
+    chips = orbs // 2
+    thin = points // LANES
+    fold = points // 2
+    tiles = chips * (chips + 1) // 2
+    block = tiles // 2 * LANES // slabs
+    f32 = jnp.float32
+    vmem = pl.BlockSpec(memory_space=pltpu.VMEM)
+    dma = pltpu.SemaphoreType.DMA
+    gath, rest, weight = pl.pallas_call(
+        functools.partial(early_kernel, slabs, orbs, (planes, rows_y, rows_z)),
+        out_shape=[
+            jax.ShapeDtypeStruct((orbs, fold, LANES), f32),
+            jax.ShapeDtypeStruct((fold, LANES), f32),
+            jax.ShapeDtypeStruct((orbs * LANES, 2 * LANES), f32),
+        ],
+        in_specs=[vmem] * 2,
+        out_specs=[vmem] * 3,
+        scratch_shapes=[pltpu.VMEM((slabs, points // slabs, LANES), f32)] * 4
+        + [
+            pltpu.VMEM((slabs, thin, LANES), f32),
+            pltpu.VMEM((9 * points // 2, LANES), f32),
+            pltpu.VMEM((9 * points // 2, LANES), f32),
+            pltpu.VMEM((points // 2, LANES), f32),
+            pltpu.VMEM((slabs * block, LANES), f32),
+            pltpu.VMEM((slabs, block, LANES), f32),
+            pltpu.VMEM((2, block, LANES), f32),
+            pltpu.VMEM((2, slabs * block, LANES), f32),
+            pltpu.VMEM((chips, panel_dev, LANES), f32),
+            pltpu.VMEM((chips, slabs, panel_dev, LANES), f32),
+            pltpu.VMEM((panel_dev, PANEL), f32),
+            pltpu.VMEM((PANEL, PANEL), f32),
+            pltpu.VMEM((PANEL, PANEL), f32),
+        ]
+        + [dma((slabs,))] * 10
+        + [dma((2, orbs))] * 2
+        + [dma((orbs,))] * 2
+        + [dma((slabs,))] * 2
+        + [dma((chips,)), dma((2,))]
+        + [dma((slabs,))] * 4
+        + [dma((chips, slabs))] * 2,
+        compiler_params=pltpu.CompilerParams(
+            collective_id=0, has_side_effects=True, vmem_limit_bytes=40 << 20
+        ),
+    )(orbitals.reshape(points, columns), potential.reshape(LANES, thin).T)
+    count = 4
+    whole = [pl.BlockSpec(memory_space=pltpu.VMEM)] * 3
+    out = pl.pallas_call(
+        final_kernel,
+        grid=(count,),
+        out_shape=jax.ShapeDtypeStruct((2, fold, LANES), f32),
+        in_specs=whole,
+        out_specs=pl.BlockSpec((2, fold // count, LANES), lambda i: (0, i, 0)),
+        scratch_shapes=[pltpu.VMEM((orbs * LANES, 2 * LANES), jnp.bfloat16)] * 2,
+        compiler_params=pltpu.CompilerParams(vmem_limit_bytes=16 << 20),
+    )(gath, rest, weight)
+    return out.reshape(planes, rows_y, rows_z, columns)
+
+
 def per_device(slabs, orbs, orbitals, potential):
     planes, rows_y, rows_z, columns = orbitals.shape
     points = planes * rows_y * rows_z
@@ -627,6 +1267,8 @@
     dma = pltpu.SemaphoreType.DMA
     steps = max(orbs // 2 - 1, 1)
     split = folds == 2 and planes == slabs and rows_y // 2 >= REACH and steps >= 2
+    if split and orbs == 8 and PANEL == 4 * LANES and 5 * LANES % (8 * slabs) == 0:
+        return early_device(slabs, orbs, orbitals, potential)
     flat = orbitals.reshape(points, columns)
     own, panel, gram, cross = pl.pallas_call(
         functools.partial(filter_kernel, slabs, orbs, (planes, rows_y, rows_z), split),

time: 139 us -> 108 us (0.78)
  Pallas kernels: 136 us -> 106 us
    pallas_call x2, Pallas kernels: 136 us -> 106 us  [the longest x1 103 us: early_device(): pl.pallas_call(functools.partial(early_kernel, slabs, orbs, (planes, rows...]
where the time goes in v1:
time: 108 us
  Pallas kernels  106 us (98%)
  local copies, waits for them, and re-layouts  2.13 us (2%)
    pallas_call x1, Pallas kernels, early_device(): pl.pallas_call(functools.partial(early_kernel, slabs, orbs, (planes, rows...  103 us
    pallas_call x1, Pallas kernels, early_device(): pl.pallas_call(final_kernel, grid=(count,), out_shape=jax.ShapeDtypeStruc...  3.42 us

profile of v1, /device:TPU:0, one launch (start us, length us, event | category | flops | bytes accessed | tf_op | source)
XLA Modules:
  0.0 108.1 jit_solution(4817713670789852442)
XLA Ops:
  0.0 0.8 reshape.10
  0.8 0.1 copy.3
  0.9 0.0 copy-start
  0.9 1.2 %copy-done = f32[4,16,32,128]{3,2,1,0:T(8,128)S(1)} copy-done((f32[4,16,32,128]{3,2,1,0:T(8,128)S(1)}, f32[4,16,32,128]{3,2,1,0:T(8,128)}, u32[]{:S(2)}) %copy-start) | copy-done | bytes 1048600
  2.1 102.5 %shard_map.28 = (f32[8,1024,128]{2,1,0:T(8,128)S(1)}, f32[1024,128]{1,0:T(8,128)S(1)}, f32[1024,256]{1,0:T(8,128)S(1)}) custom-call(f32[2048,128]{1,0:T(8,128)S(1)} %bitcast.3, f32[16,128]{1,0:T(8,128)S(1)} %bitcast.4), custom_call_target="tpu_custom_call" | custom-call | tf_op jit(solution)/shard_map/pallas_call | solution.py:1209
  104.7 3.4 %shard_map.29 = f32[2,1024,128]{2,1,0:T(8,128)} custom-call(f32[8,1024,128]{2,1,0:T(8,128)S(1)} %get-tuple-element.8.gath_ref, f32[1024,128]{1,0:T(8,128)S(1)} %get-tuple-element.9.rest_ref, f32[1024,256]{1,0:T(8,128)S(1)} %get-tuple-element.10.weight_ref), custom_call_target="tpu_custom_call" | custom-call | tf_op jit(solution)/shard_map/pallas_call | solution.py:1247
Async XLA Ops:
  0.9 1.2 %copy-start = (f32[4,16,32,128]{3,2,1,0:T(8,128)S(1)}, f32[4,16,32,128]{3,2,1,0:T(8,128)}, u32[]{:S(2)}) copy-start(f32[4,16,32,128]{3,2,1,0:T(8,128)} %param.2) | copy-start | bytes 3145732

commit v2 on v1

--- a/solution.py
+++ b/solution.py
@@ -644,10 +644,27 @@
 
 
 def link_orders():
-    up = {0: [(0, 1), (0, 0)], 1: [(1, 1), (0, 1), (1, 0), (0, 0)],
-          2: [(2, 1), (2, 0), (1, 1), (0, 1), (1, 0), (0, 0)]}
-    down = {3 - z: [(3 - o, 1 - h) for o, h in order] for z, order in up.items()}
-    return up, down
+    def both(table):
+        out = {z: list(items) for z, items in table.items()}
+        for z, items in table.items():
+            out[3 - z] = [(1 - way, 3 - o, 1 - h) for way, o, h in items]
+        return out
+
+    starts = both({0: [(0, 0, 0), (0, 0, 1)], 1: [(0, 1, 1), (1, 1, 0), (1, 1, 1)]})
+    arrive = [
+        both({0: [(1, 1, 0), (1, 1, 1)], 1: [(0, 0, 0), (1, 2, 0), (1, 3, 0)]}),
+        both({0: [(1, 2, 0)], 1: [(0, 0, 1), (1, 2, 1)]}),
+        both({0: [(1, 3, 0)], 1: [(1, 3, 1)]}),
+        both({0: [(1, 2, 1)]}),
+        both({0: [(1, 3, 1)]}),
+    ]
+    passed = [
+        both({1: [(0, 1, 0), (1, 2, 0)]}),
+        both({1: [(0, 0, 0), (1, 3, 0)]}),
+        both({1: [(1, 2, 1)]}),
+        both({1: [(1, 3, 1)]}),
+    ]
+    return starts, arrive, passed
 
 
 def early_kernel(
@@ -656,7 +673,7 @@
     pack, land, pack_back, land_back, pot_land, wide_a, wide_b, level,
     gram_part, gram_land, gram_chip, gram_all, cross_part, cross_land, cross, work, inverse,
     a_send, a_recv, p_send, p_recv, b_send, b_recv, e_send, e_recv, f_send, f_recv,
-    along_send, along_recv, across_send, across_recv,
+    along_send, along_recv, direct_send, across_send, across_recv,
     r_send, r_recv, z_send, z_recv, s_send, s_recv, t_send, t_recv, c_send, c_recv,
 ):
     planes, rows_y, rows_z = shape
@@ -754,9 +771,11 @@
 
         lax.fori_loop(0, rows_y // 2, body, 0)
 
-    def filter_half(h, during=None):
+    def filter_half(h):
         with jax.named_scope("wait_a"):
             wait(pack, land, h, out_sems)
+        if h == 0:
+            send(pack, land, 1, out_sems)
 
         def unpack(at):
             parts = [land[i, pl.ds(h * rows + at, step), :] for i in range(slabs)]
@@ -768,9 +787,7 @@
         with jax.named_scope("sweep"):
             sweep(wide_a, wide_b, True)
             source, target = wide_b, wide_a
-            for order in range(DEGREE - 1):
-                if during and order == DEGREE - 2:
-                    during()
+            for _ in range(DEGREE - 1):
                 sweep(source, target, False)
                 source, target = target, source
 
@@ -783,7 +800,6 @@
 
         with jax.named_scope("pack_b"):
             over(body)
-            send(pack_back, land_back, h, back_sems)
 
     def fold_half(h, store):
         with jax.named_scope("wait_b"):
@@ -808,7 +824,6 @@
     send(pack, land, 0, out_sems)
     with jax.named_scope("pack"):
         pack_half(1)
-    send(pack, land, 1, out_sems)
     pot_land[here] = pot_ref[...]
     with jax.named_scope("level"):
         wait_exchange(slabs, here, p_send, p_recv, lambda there: pot_ref, pot_land)
@@ -825,9 +840,9 @@
                     value - (SHIFT_MID + 1.5 * STENCIL[0])
                 ) * (1.0 / HALF_WIDTH)
 
-    up, down = link_orders()
-
-    def along(origin, h, way):
+    starts, arrive, passed = link_orders()
+
+    def along(way, origin, h):
         view = gath.at[origin * 2 + core, h * part_rows : (h + 1) * part_rows]
         return pltpu.make_async_remote_copy(
             src_ref=view,
@@ -835,6 +850,18 @@
             send_sem=along_send.at[way, origin * 2 + h],
             recv_sem=along_recv.at[way, origin * 2 + h],
             device_id={"orb": (chip + 1 - 2 * way) * 2 + core},
+            device_id_type=MESH,
+        )
+
+    def direct(z):
+        way, h = (0, 1) if z == 0 else (1, 0)
+        view = gath.at[z * 2 + core, h * part_rows : (h + 1) * part_rows]
+        return pltpu.make_async_remote_copy(
+            src_ref=view,
+            dst_ref=view,
+            send_sem=direct_send.at[0],
+            recv_sem=along_recv.at[way, z * 2 + h],
+            device_id={"orb": (z + 2 - 4 * way) * 2 + core},
             device_id_type=MESH,
         )
 
@@ -852,84 +879,50 @@
     def on_chip(z, body):
         pl.when(chip == z)(body)
 
-    def arrivals(z, t):
-        found = []
-        for way, orders in ((0, up), (1, down)):
-            order = orders.get(z - 1 + 2 * way, [])
-            if t < len(order):
-                found.append((way, order[t]))
-        return found
+    def by_chip(table, body):
+        for z in table:
+            def run():
+                for item in table[z]:
+                    body(*item)
+
+            on_chip(z, run)
+
+    own_items = {z: [(0, z, h) for h in range(2)] for z in range(chips)}
 
     def begin():
-        for z in range(chips):
-            def body():
-                for way, orders in ((0, up), (1, down)):
-                    if z in orders:
-                        for item in orders[z]:
-                            if item[0] != z:
-                                break
-                            along(*item, way).start()
-                for h in range(2):
-                    across(z, h, core).start()
-
-            on_chip(z, body)
+        for z in (0, chips - 1):
+            on_chip(z, lambda: direct(z).start())
+        by_chip(starts, lambda *item: along(*item).start())
+        by_chip(own_items, lambda way, o, h: across(o, h, core).start())
 
     def receive(t):
+        def one(way, o, h):
+            along(way, o, h).wait_recv()
+            across(o, h, core).start()
+
         with jax.named_scope("receive"):
-            for z in range(chips):
-                def body():
-                    for way, item in arrivals(z, t):
-                        along(*item, way).wait_recv()
-                        across(*item, core).start()
-
-                on_chip(z, body)
+            by_chip(arrive[t], one)
 
     def forward(t):
-        for z in range(chips):
-            def body():
-                for way, item in arrivals(z, t):
-                    order = (up, down)[way].get(z, [])
-                    if item in order:
-                        along(*item, way).start()
-                        for later in order[order.index(item) + 1 :]:
-                            if later[0] != z:
-                                break
-                            along(*later, way).start()
-
-            on_chip(z, body)
+        by_chip(passed[t], lambda *item: along(*item).start())
 
     def settle(t):
         with jax.named_scope("settle"):
-            for z in range(chips):
-                def body():
-                    for way, item in arrivals(z, t):
-                        across(*item, 1 - core).wait_recv()
-
-                on_chip(z, body)
+            by_chip(arrive[t], lambda way, o, h: across(o, h, 1 - core).wait_recv())
 
     def settle_own():
-        for z in range(chips):
-            def body():
-                for h in range(2):
-                    across(z, h, 1 - core).wait_recv()
-
-            on_chip(z, body)
+        by_chip(own_items, lambda way, o, h: across(o, h, 1 - core).wait_recv())
 
     def drain():
-        for z in range(chips):
-            def body():
-                for way, orders in ((0, up), (1, down)):
-                    for item in orders.get(z, []):
-                        along(*item, way).wait_send()
-                for h in range(2):
-                    across(z, h, core).wait_send()
-                for t in range(2 * (chips - 1)):
-                    for way, item in arrivals(z, t):
-                        across(*item, core).wait_send()
-
-            on_chip(z, body)
+        for z in (0, chips - 1):
+            on_chip(z, lambda: direct(z).wait_send())
+        for table in [starts] + passed:
+            by_chip(table, lambda *item: along(*item).wait_send())
+        for table in [own_items] + arrive:
+            by_chip(table, lambda way, o, h: across(o, h, core).wait_send())
 
     filter_half(0)
+    send(pack_back, land_back, 0, back_sems)
 
     def store_panel(at, value):
         gath[me, at, :] = value
@@ -937,15 +930,11 @@
     fold_half(0, store_panel)
     begin()
 
-    def first():
-        receive(0)
-        forward(0)
-
-    filter_half(1, first)
-    receive(1)
+    filter_half(1)
+    receive(0)
+    forward(0)
     settle_own()
     settle(0)
-    settle(1)
 
     tiles = chips * (chips + 1) // 2
     share = tiles // 2
@@ -975,10 +964,7 @@
             lax.fori_loop(0, share, tile, 0)
         exchange(slabs, here, r_send, r_recv, lambda there: gram_part.at[block_at(there)], gram_land)
 
-    def store_rest(at, value):
-        rest_ref[at, :] = value
-
-    fold_half(1, store_rest)
+    send(pack_back, land_back, 1, back_sems)
 
     def spread(index, there):
         view = gram_chip.at[index]
@@ -1009,27 +995,6 @@
 
         on_chip(z, body)
     forward(1)
-    receive(2)
-    forward(2)
-
-    def couple(n, z):
-        rows_k = 256
-        with jax.named_scope("couple"):
-            def product(k, total):
-                at = pl.ds(pl.multiple_of(k * rows_k, rows_k), rows_k)
-                return total + dot_pieces(pieces(rest_ref[at, :]), pieces(pair(z, at)), (0, 0))
-
-            total = lax.fori_loop(
-                0, fold // rows_k, product, jnp.zeros((LANES, 2 * LANES), jnp.float32)
-            )
-            value = unfolded(total, 1)[0]
-            cross_part[n] = value
-            cross_land[n, here] = value
-        exchange(slabs, here, c_send.at[n], c_recv.at[n], lambda there: cross_part.at[n], cross_land.at[n])
-
-    lower = chip // 2
-    order = [chip, chip + 1 - 2 * lax.rem(chip, 2), 2 - lower, 3 - 3 * lower]
-    couple(0, order[0])
 
     with jax.named_scope("wait_z"):
         for z in range(chips):
@@ -1045,9 +1010,6 @@
             on_chip(z, body)
     gram_all[core, block_at(here), :] = gram_chip[0] + gram_chip[1]
 
-    def own_block(there):
-        return gram_all.at[core, block_at(here)]
-
     def gram_side(side, s):
         view = gram_all.at[side, block_at(s)]
         return pltpu.make_async_remote_copy(
@@ -1073,14 +1035,39 @@
     for hop in range(1, slabs):
         plane_copy(hop, here, lax.rem(here + hop, slabs)).start()
     gram_side(core, here).start()
-    couple(1, order[1])
-    receive(3)
-    forward(3)
+
+    def store_rest(at, value):
+        rest_ref[at, :] = value
+
+    fold_half(1, store_rest)
+
+    def couple(n, z):
+        rows_k = 256
+        with jax.named_scope("couple"):
+            def product(k, total):
+                at = pl.ds(pl.multiple_of(k * rows_k, rows_k), rows_k)
+                return total + dot_pieces(pieces(rest_ref[at, :]), pieces(pair(z, at)), (0, 0))
+
+            total = lax.fori_loop(
+                0, fold // rows_k, product, jnp.zeros((LANES, 2 * LANES), jnp.float32)
+            )
+            value = unfolded(total, 1)[0]
+            cross_part[n] = value
+            cross_land[n, here] = value
+        exchange(slabs, here, c_send.at[n], c_recv.at[n], lambda there: cross_part.at[n], cross_land.at[n])
+
+    lower = chip // 2
+    order = [chip, chip + 1 - 2 * lax.rem(chip, 2), 2 - lower, 3 - 3 * lower]
+    receive(1)
+    forward(2)
     with jax.named_scope("wait_s"):
         for hop in range(1, slabs):
             source = lax.rem(here + slabs - hop, slabs)
             plane_copy(hop, source, lax.rem(here + hop, slabs)).wait_recv()
             gram_side(core, source).start()
+    couple(0, order[0])
+    settle(1)
+    with jax.named_scope("wait_t"):
         for s in range(slabs):
             gram_side(1 - core, s).wait_recv()
 
@@ -1117,20 +1104,21 @@
 
         @pl.when(b == 0)
         def _():
-            receive(4)
-            forward(4)
+            receive(2)
+            forward(3)
+            couple(1, order[1])
+            receive(3)
 
         @pl.when(b == 1)
         def _():
             settle(2)
             settle(3)
-            settle(4)
             couple(2, order[2])
+            receive(4)
 
         @pl.when(b == 2)
         def _():
-            receive(5)
-            settle(5)
+            settle(4)
             couple(3, order[3])
 
         return carry
@@ -1233,6 +1221,7 @@
         ]
         + [dma((slabs,))] * 10
         + [dma((2, orbs))] * 2
+        + [dma((1,))]
         + [dma((orbs,))] * 2
         + [dma((slabs,))] * 2
         + [dma((chips,)), dma((2,))]

time: 108 us -> 106 us (0.981)
  Pallas kernels: 106 us -> 103 us
    pallas_call x1, Pallas kernels: 103 us -> 100 us  [early_device(): pl.pallas_call(functools.partial(early_kernel, slabs, orbs, (planes, rows...]
where the time goes in v2:
time: 106 us
  Pallas kernels  103 us (97%)
  local copies, waits for them, and re-layouts  2.13 us (2%)
    pallas_call x1, Pallas kernels, early_device(): pl.pallas_call(functools.partial(early_kernel, slabs, orbs, (planes, rows...  100 us
    pallas_call x1, Pallas kernels, early_device(): pl.pallas_call(final_kernel, grid=(count,), out_shape=jax.ShapeDtypeStruc...  3.41 us

profile of v2, /device:TPU:0, one launch (start us, length us, event | category | flops | bytes accessed | tf_op | source)
XLA Modules:
  0.0 105.6 jit_solution(1920500401286058839)
XLA Ops:
  0.0 0.8 reshape.10
  0.8 0.1 copy.3
  0.9 0.0 copy-start
  0.9 1.2 %copy-done = f32[4,16,32,128]{3,2,1,0:T(8,128)S(1)} copy-done((f32[4,16,32,128]{3,2,1,0:T(8,128)S(1)}, f32[4,16,32,128]{3,2,1,0:T(8,128)}, u32[]{:S(2)}) %copy-start) | copy-done | bytes 1048600
  2.1 100.1 %shard_map.28 = (f32[8,1024,128]{2,1,0:T(8,128)S(1)}, f32[1024,128]{1,0:T(8,128)S(1)}, f32[1024,256]{1,0:T(8,128)S(1)}) custom-call(f32[2048,128]{1,0:T(8,128)S(1)} %bitcast.3, f32[16,128]{1,0:T(8,128)S(1)} %bitcast.4), custom_call_target="tpu_custom_call" | custom-call | tf_op jit(solution)/shard_map/pallas_call | solution.py:1197
  102.2 3.4 %shard_map.29 = f32[2,1024,128]{2,1,0:T(8,128)} custom-call(f32[8,1024,128]{2,1,0:T(8,128)S(1)} %get-tuple-element.8.gath_ref, f32[1024,128]{1,0:T(8,128)S(1)} %get-tuple-element.9.rest_ref, f32[1024,256]{1,0:T(8,128)S(1)} %get-tuple-element.10.weight_ref), custom_call_target="tpu_custom_call" | custom-call | tf_op jit(solution)/shard_map/pallas_call | solution.py:1236
Async XLA Ops:
  0.9 1.2 %copy-start = (f32[4,16,32,128]{3,2,1,0:T(8,128)S(1)}, f32[4,16,32,128]{3,2,1,0:T(8,128)}, u32[]{:S(2)}) copy-start(f32[4,16,32,128]{3,2,1,0:T(8,128)} %param.2) | copy-start | bytes 3145732

commit v3 on v2

--- a/solution.py
+++ b/solution.py
@@ -650,16 +650,21 @@
             out[3 - z] = [(1 - way, 3 - o, 1 - h) for way, o, h in items]
         return out
 
-    starts = both({0: [(0, 0, 0), (0, 0, 1)], 1: [(0, 1, 1), (1, 1, 0), (1, 1, 1)]})
+    starts = [
+        {0: [(0, 0, 0)], 1: [(1, 1, 0)], 2: [(1, 2, 0), (0, 2, 0)]},
+        {0: [(0, 0, 1)], 1: [(0, 1, 1), (1, 1, 1)], 2: [(0, 2, 1)], 3: [(1, 3, 1), (1, 3, 0)]},
+    ]
     arrive = [
-        both({0: [(1, 1, 0), (1, 1, 1)], 1: [(0, 0, 0), (1, 2, 0), (1, 3, 0)]}),
+        both({1: [(1, 2, 0)]}),
+        both({0: [(1, 1, 0), (1, 1, 1)], 1: [(0, 0, 0), (1, 3, 0)]}),
         both({0: [(1, 2, 0)], 1: [(0, 0, 1), (1, 2, 1)]}),
         both({0: [(1, 3, 0)], 1: [(1, 3, 1)]}),
         both({0: [(1, 2, 1)]}),
         both({0: [(1, 3, 1)]}),
     ]
     passed = [
-        both({1: [(0, 1, 0), (1, 2, 0)]}),
+        both({1: [(1, 2, 0)]}),
+        both({1: [(0, 1, 0)]}),
         both({1: [(0, 0, 0), (1, 3, 0)]}),
         both({1: [(1, 2, 1)]}),
         both({1: [(1, 3, 1)]}),
@@ -667,12 +672,81 @@
     return starts, arrive, passed
 
 
+def tile_inverse(a):
+    n = LANES
+    tiles = n // 8
+    rows = lax.broadcasted_iota(jnp.int32, (8, n), 0)
+    lanes = lax.broadcasted_iota(jnp.int32, (8, n), 1)
+
+    def row_of(value, k):
+        return jnp.broadcast_to(value[k : k + 1], (8, n))
+
+    def column_of(value, k):
+        return jnp.broadcast_to(value[:, k : k + 1], (8, n))
+
+    def tree(terms):
+        while len(terms) > 1:
+            paired = [terms[i] + terms[i + 1] for i in range(0, len(terms) - 1, 2)]
+            terms = paired + terms[len(terms) - len(terms) % 2 :]
+        return terms[0]
+
+    work = [a[8 * t : 8 * t + 8] for t in range(tiles)]
+    cols = [column_of(work[0], k) for k in range(8)]
+    out = []
+    for t0 in range(tiles):
+        base = 8 * t0
+        last = t0 == tiles - 1
+        if not last:
+            side = [column_of(work[t0 + 1], base + k) for k in range(8)]
+            ahead = [column_of(work[t0 + 1], base + 8 + k) for k in range(8)]
+            moved = list(side)
+        below, pivots, scales = [], [], []
+        for j in range(8):
+            pivot = row_of(cols[j], j)
+            scale = 1.0 / pivot
+            lead = jnp.where(rows > j, cols[j], 0.0)
+            pivots.append(pivot)
+            scales.append(scale)
+            below.append(lead * scale)
+            for k in range(j + 1, 8):
+                part = row_of(cols[k], j) * scale
+                cols[k] = cols[k] - lead * part
+                if not last:
+                    moved[k] = moved[k] - moved[j] * part
+        above = cols
+        if not last:
+            scaled = [moved[j] * scales[j] for j in range(8)]
+            cols = [
+                ahead[k] - tree([scaled[j] * row_of(moved[j], k) for j in range(8)]) for k in range(8)
+            ]
+        inside = (lanes >= base) & (lanes < base + 8)
+        value = jnp.where(inside, jnp.where(lanes == rows + base, 1.0, 0.0), work[t0])
+        root, turn = pivots[0], scales[0]
+        for j in range(8):
+            value = value - below[j] * row_of(value, j)
+            if j:
+                root = jnp.where(rows == j, pivots[j], root)
+                turn = jnp.where(rows == j, scales[j], turn)
+        out.append(jnp.where(lanes < base + 8, value * lax.rsqrt(root), 0.0))
+        if last:
+            break
+        value = value * turn
+        for k in range(7, 0, -1):
+            value = value - jnp.where(rows < k, above[k] * turn, 0.0) * row_of(value, k)
+        leads = [row_of(value, k) for k in range(8)]
+        for t in range(t0 + 1, tiles):
+            before = work[t]
+            columns = side if t == t0 + 1 else [column_of(before, base + k) for k in range(8)]
+            work[t] = jnp.where(inside, 0.0, before) - tree([columns[k] * leads[k] for k in range(8)])
+    return jnp.concatenate(out, axis=0)
+
+
 def early_kernel(
     slabs, orbs, shape,
-    x_ref, pot_ref, gath, rest_ref, weight_ref,
-    pack, land, pack_back, land_back, pot_land, wide_a, wide_b, level,
+    x_hbm, pot_ref, gath, rest_ref, weight_ref,
+    x_ref, pot_wide, pot_mine, pack, land, pack_back, land_back, pot_land, wide_a, wide_b, level,
     gram_part, gram_land, gram_chip, gram_all, cross_part, cross_land, cross, work, inverse,
-    a_send, a_recv, p_send, p_recv, b_send, b_recv, e_send, e_recv, f_send, f_recv,
+    x_sem, a_send, a_recv, p_send, p_recv, b_send, b_recv,
     along_send, along_recv, direct_send, across_send, across_recv,
     r_send, r_recv, z_send, z_recv, s_send, s_recv, t_send, t_recv, c_send, c_recv,
 ):
@@ -686,14 +760,20 @@
     width = LANES // slots
     rows = points // slots
     plane = 3 * rows
-    thin = points // LANES
+    sub = rows // 2
     fold = points // 2
     part_rows = fold // 2
     panel_dev = PANEL // orbs
     points_all = points * slabs
     step = 16
     slot = lax.broadcasted_iota(jnp.int32, (step, LANES), 1) // width
-    out_sems, back_sems = ((a_send, a_recv), (e_send, e_recv)), ((b_send, b_recv), (f_send, f_recv))
+
+    def fetch(c):
+        view = slice(c * sub, (c + 1) * sub)
+        return pltpu.make_async_copy(x_hbm.at[:, view], x_ref.at[:, view], x_sem.at[c])
+
+    for c in range(2):
+        fetch(c).start()
 
     barrier = pltpu.get_barrier_semaphore()
     for hop in range(1, slabs):
@@ -713,30 +793,39 @@
             out = value if out is None else jnp.where(slot == u, value, out)
         return out
 
-    def over(body):
+    def over(c, body):
         def one(block, carry):
-            body(pl.multiple_of(block * step, step))
+            body(pl.multiple_of(c * sub + block * step, step))
             return carry
 
-        lax.fori_loop(0, rows // step, one, 0)
-
-    def half(buf, h):
-        return buf.at[:, h * rows : (h + 1) * rows]
-
-    def send(buf, landing, h, sems):
-        exchange(slabs, here, *sems[h], lambda there: half(buf, h).at[there], half(landing, h))
-        landing[here, h * rows : (h + 1) * rows] = buf[here, h * rows : (h + 1) * rows]
-
-    def wait(buf, landing, h, sems):
-        wait_exchange(slabs, here, *sems[h], lambda there: half(buf, h).at[there], half(landing, h))
-
-    def pack_half(h):
+        lax.fori_loop(0, sub // step, one, 0)
+
+    def span(h, c):
+        return slice(h * rows + c * sub, h * rows + (c + 1) * sub)
+
+    def send(buf, landing, h, c, sems):
+        at, k = span(h, c), h * 2 + c
+        exchange(
+            slabs, here, sems[0].at[k], sems[1].at[k], lambda there: buf.at[there, at], landing.at[:, at]
+        )
+        landing[here, at] = buf[here, at]
+
+    def wait(buf, landing, h, c, sems):
+        at, k = span(h, c), h * 2 + c
+        wait_exchange(
+            slabs, here, sems[0].at[k], sems[1].at[k], lambda there: buf.at[there, at], landing.at[:, at]
+        )
+
+    out_sems, back_sems = (a_send, a_recv), (b_send, b_recv)
+
+    def pack_part(h, c):
         def body(at):
-            parts = [x_ref[pl.ds(q * rows + at, step), :] for q in range(slots)]
+            parts = [x_ref[q, pl.ds(at, step), :] for q in range(slots)]
             for j in range(slabs):
                 pack[j, pl.ds(h * rows + at, step), :] = merge([(part, h * slabs + j) for part in parts])
 
-        over(body)
+        with jax.named_scope("pack"):
+            over(c, body)
 
     def put(target, p, row, value):
         odd = lax.rem(lax.broadcasted_iota(jnp.int32, value.shape, 1) // width, 2)
@@ -750,7 +839,7 @@
 
     taps = [-0.5 * c / HALF_WIDTH for c in STENCIL]
 
-    def sweep(source, target, first):
+    def sweep(source, target, first, low=0, high=rows_y // 2):
         def body(y, carry):
             for p in range(planes):
                 def line(q, yy):
@@ -769,74 +858,86 @@
                 put(target, p, row, total)
             return carry
 
-        lax.fori_loop(0, rows_y // 2, body, 0)
-
-    def filter_half(h):
-        with jax.named_scope("wait_a"):
-            wait(pack, land, h, out_sems)
-        if h == 0:
-            send(pack, land, 1, out_sems)
-
-        def unpack(at):
-            parts = [land[i, pl.ds(h * rows + at, step), :] for i in range(slabs)]
-            for p in range(planes):
-                put(wide_a, p, at, merge([(parts[u // 2], 2 * p + u % 2) for u in range(slots)]))
-
-        with jax.named_scope("unpack"):
-            over(unpack)
+        lax.fori_loop(low, high, body, 0)
+
+    def filter_half(h, during, ready):
+        for c in range(2):
+            with jax.named_scope("wait_a"):
+                wait(pack, land, h, c, out_sems)
+
+            def unpack(at):
+                parts = [land[i, pl.ds(h * rows + at, step), :] for i in range(slabs)]
+                for p in range(planes):
+                    put(wide_a, p, at, merge([(parts[u // 2], 2 * p + u % 2) for u in range(slots)]))
+
+            with jax.named_scope("unpack"):
+                over(c, unpack)
+        during[0]()
+        source, target = wide_a, wide_b
         with jax.named_scope("sweep"):
-            sweep(wide_a, wide_b, True)
-            source, target = wide_b, wide_a
-            for _ in range(DEGREE - 1):
-                sweep(source, target, False)
+            for order in range(DEGREE - 1):
+                if order == 2:
+                    during[1]()
+                sweep(source, target, order == 0)
                 source, target = target, source
-
-        def body(at):
-            parts = [source[pl.ds((planes + p) * plane + rows + at, step), :] for p in range(planes)]
-            for i in range(slabs):
-                pack_back[i, pl.ds(h * rows + at, step), :] = merge(
-                    [(parts[q // 2], 2 * i + q % 2) for q in range(slots)]
-                )
-
-        with jax.named_scope("pack_b"):
-            over(body)
-
-    def fold_half(h, store):
+        for c in range(2):
+            with jax.named_scope("sweep"):
+                sweep(source, target, False, c * rows_y // 4, (c + 1) * rows_y // 4)
+
+            def body(at):
+                parts = [target[pl.ds((planes + p) * plane + rows + at, step), :] for p in range(planes)]
+                for i in range(slabs):
+                    pack_back[i, pl.ds(h * rows + at, step), :] = merge(
+                        [(parts[q // 2], 2 * i + q % 2) for q in range(slots)]
+                    )
+
+            with jax.named_scope("pack_b"):
+                over(c, body)
+            ready(c)
+
+    def fold_part(h, c, store):
         with jax.named_scope("wait_b"):
-            wait(pack_back, land_back, h, back_sems)
+            wait(pack_back, land_back, h, c, back_sems)
 
         def body(at):
             parts = [land_back[j, pl.ds(h * rows + at, step), :] for j in range(slabs)]
             for k in range(slabs):
+                row = pl.multiple_of(c * part_rows + k * sub + at - c * sub, step)
                 store(
-                    pl.ds(k * rows + at, step),
+                    pl.ds(row, step),
                     merge([(parts[u % slabs], (u // slabs) * slabs + k) for u in range(slots)]),
                 )
 
         with jax.named_scope("fold"):
-            over(body)
-
-    with jax.named_scope("pack"):
-        pack_half(0)
+            over(c, body)
+
+    pot_wide[...] = jnp.zeros_like(pot_wide)
+    pot_wide[: planes * rows_y, :rows_z] = pot_ref[...]
+    pot_mine[...] = pot_wide[...].T[:rows_z]
+    fetch(0).wait()
+    pack_part(0, 0)
     with jax.named_scope("barrier"):
         pl.semaphore_wait(barrier, slabs - 1 + orbs - 1)
-    exchange(slabs, here, p_send, p_recv, lambda there: pot_ref, pot_land)
-    send(pack, land, 0, out_sems)
-    with jax.named_scope("pack"):
-        pack_half(1)
-    pot_land[here] = pot_ref[...]
+    exchange(slabs, here, p_send, p_recv, lambda there: pot_mine, pot_land)
+    send(pack, land, 0, 0, out_sems)
+    fetch(1).wait()
+    pack_part(0, 1)
+    send(pack, land, 0, 1, out_sems)
+    for c in range(2):
+        pack_part(1, c)
+    pot_land[here] = pot_mine[...]
     with jax.named_scope("level"):
-        wait_exchange(slabs, here, p_send, p_recv, lambda there: pot_ref, pot_land)
-        lane_slot = lax.broadcasted_iota(jnp.int32, (thin, LANES), 1) // width
+        wait_exchange(slabs, here, p_send, p_recv, lambda there: pot_mine, pot_land)
+        lane_slot = lax.broadcasted_iota(jnp.int32, (rows_z, LANES), 1) // width
         fields = [pot_land[s] for s in range(slabs)]
         for p in range(planes):
-            for e in range(rows // thin):
+            for y in range(rows_y // 2):
                 value = None
                 for u in range(slots):
-                    l = (2 * p + u % 2) * (rows // thin) + e
-                    spread = jnp.broadcast_to(fields[u // 2][:, l : l + 1], (thin, LANES))
+                    l = p * rows_y + u % 2 * (rows_y // 2) + y
+                    spread = jnp.broadcast_to(fields[u // 2][:, l : l + 1], (rows_z, LANES))
                     value = spread if value is None else jnp.where(lane_slot == u, spread, value)
-                level[pl.ds(p * rows + e * thin, thin), :] = (
+                level[pl.ds(p * rows + y * rows_z, rows_z), :] = (
                     value - (SHIFT_MID + 1.5 * STENCIL[0])
                 ) * (1.0 / HALF_WIDTH)
 
@@ -889,11 +990,11 @@
 
     own_items = {z: [(0, z, h) for h in range(2)] for z in range(chips)}
 
-    def begin():
-        for z in (0, chips - 1):
-            on_chip(z, lambda: direct(z).start())
-        by_chip(starts, lambda *item: along(*item).start())
-        by_chip(own_items, lambda way, o, h: across(o, h, core).start())
+    def begin(c):
+        on_chip((chips - 1) * (1 - c), lambda: direct((chips - 1) * (1 - c)).start())
+        by_chip(starts[c], lambda *item: along(*item).start())
+        for z in range(chips):
+            on_chip(z, lambda: across(z, c, core).start())
 
     def receive(t):
         def one(way, o, h):
@@ -916,25 +1017,36 @@
     def drain():
         for z in (0, chips - 1):
             on_chip(z, lambda: direct(z).wait_send())
-        for table in [starts] + passed:
+        for table in starts + passed:
             by_chip(table, lambda *item: along(*item).wait_send())
         for table in [own_items] + arrive:
             by_chip(table, lambda way, o, h: across(o, h, core).wait_send())
 
-    filter_half(0)
-    send(pack_back, land_back, 0, back_sems)
+    def send_trailing():
+        for c in range(2):
+            send(pack, land, 1, c, out_sems)
+
+    filter_half(
+        0, (send_trailing, lambda: None), lambda c: send(pack_back, land_back, 0, c, back_sems)
+    )
 
     def store_panel(at, value):
         gath[me, at, :] = value
 
-    fold_half(0, store_panel)
-    begin()
-
-    filter_half(1)
-    receive(0)
-    forward(0)
+    for c in range(2):
+        fold_part(0, c, store_panel)
+        begin(c)
+
+    def early():
+        receive(0)
+        forward(0)
+
+    filter_half(1, (lambda: None, early), lambda c: None)
+    receive(1)
+    forward(1)
     settle_own()
     settle(0)
+    settle(1)
 
     tiles = chips * (chips + 1) // 2
     share = tiles // 2
@@ -964,7 +1076,8 @@
             lax.fori_loop(0, share, tile, 0)
         exchange(slabs, here, r_send, r_recv, lambda there: gram_part.at[block_at(there)], gram_land)
 
-    send(pack_back, land_back, 1, back_sems)
+    for c in range(2):
+        send(pack_back, land_back, 1, c, back_sems)
 
     def spread(index, there):
         view = gram_chip.at[index]
@@ -994,7 +1107,7 @@
                     spread(z - 1, there).start()
 
         on_chip(z, body)
-    forward(1)
+    forward(2)
 
     with jax.named_scope("wait_z"):
         for z in range(chips):
@@ -1039,40 +1152,46 @@
     def store_rest(at, value):
         rest_ref[at, :] = value
 
-    fold_half(1, store_rest)
+    for c in range(2):
+        fold_part(1, c, store_rest)
+
+    def couple_part(z, k):
+        at = pl.ds(pl.multiple_of(k * 2 * LANES, 2 * LANES), 2 * LANES)
+        return dot_pieces(pieces(rest_ref[at, :]), pieces(pair(z, at)), (0, 0))
+
+    def couple_send(n, total):
+        value = unfolded(total, 1)[0]
+        cross_part[n] = value
+        cross_land[n, here] = value
+        exchange(slabs, here, c_send.at[n], c_recv.at[n], lambda there: cross_part.at[n], cross_land.at[n])
 
     def couple(n, z):
-        rows_k = 256
         with jax.named_scope("couple"):
-            def product(k, total):
-                at = pl.ds(pl.multiple_of(k * rows_k, rows_k), rows_k)
-                return total + dot_pieces(pieces(rest_ref[at, :]), pieces(pair(z, at)), (0, 0))
-
             total = lax.fori_loop(
-                0, fold // rows_k, product, jnp.zeros((LANES, 2 * LANES), jnp.float32)
+                0, fold // (2 * LANES), lambda k, total: total + couple_part(z, k),
+                jnp.zeros((LANES, 2 * LANES), jnp.float32),
             )
-            value = unfolded(total, 1)[0]
-            cross_part[n] = value
-            cross_land[n, here] = value
-        exchange(slabs, here, c_send.at[n], c_recv.at[n], lambda there: cross_part.at[n], cross_land.at[n])
+        couple_send(n, total)
 
     lower = chip // 2
     order = [chip, chip + 1 - 2 * lax.rem(chip, 2), 2 - lower, 3 - 3 * lower]
-    receive(1)
-    forward(2)
+    receive(2)
+    forward(3)
     with jax.named_scope("wait_s"):
         for hop in range(1, slabs):
             source = lax.rem(here + slabs - hop, slabs)
             plane_copy(hop, source, lax.rem(here + hop, slabs)).wait_recv()
             gram_side(core, source).start()
     couple(0, order[0])
-    settle(1)
+    settle(2)
+    receive(3)
+    forward(4)
+    couple(1, order[1])
     with jax.named_scope("wait_t"):
         for s in range(slabs):
             gram_side(1 - core, s).wait_recv()
 
     n = LANES
-    blocks = chips
     inverse[...] = jnp.zeros_like(inverse)
     for za in range(chips):
         for zb in range(za + 1):
@@ -1081,57 +1200,44 @@
                 t // share, (t % share) * n : (t % share + 1) * n, :
             ]
 
-    def factor(b, carry):
-        at = pl.multiple_of(b * n, n)
+    def between(b):
+        if b == 0:
+            receive(4)
+        if b == 1:
+            settle(3)
+            settle(4)
+        if b == 2:
+            receive(5)
+            settle(5)
+            couple(3, order[3])
+
+    for b in range(chips):
+        at, past = slice(b * n, (b + 1) * n), slice((b + 1) * n, PANEL)
         with jax.named_scope("diag"):
-            diag = block_inverse(work[pl.ds(at, n), pl.ds(at, n)])
-            inverse[pl.ds(at, n), pl.ds(at, n)] = diag
-        for i in range(1, blocks):
-            @pl.when(i > b)
-            def _():
-                work[i * n : (i + 1) * n, pl.ds(at, n)] = dot(
-                    work[i * n : (i + 1) * n, pl.ds(at, n)], diag, (1, 1)
-                )
-        for i in range(1, blocks):
-            @pl.when(i > b)
-            def _():
-                left = work[i * n : (i + 1) * n, pl.ds(at, n)]
-                for k in range(1, i + 1):
-                    @pl.when(k > b)
-                    def _():
-                        right = work[k * n : (k + 1) * n, pl.ds(at, n)]
-                        work[i * n : (i + 1) * n, k * n : (k + 1) * n] -= dot(left, right, (1, 1))
-
-        @pl.when(b == 0)
-        def _():
-            receive(2)
-            forward(3)
-            couple(1, order[1])
-            receive(3)
-
-        @pl.when(b == 1)
-        def _():
-            settle(2)
-            settle(3)
-            couple(2, order[2])
-            receive(4)
-
-        @pl.when(b == 2)
-        def _():
-            settle(4)
-            couple(3, order[3])
-
-        return carry
-
-    with jax.named_scope("factor"):
-        lax.fori_loop(0, blocks, factor, 0)
-    with jax.named_scope("inverse"):
-        for i in range(1, blocks):
-            span = i * n
-            inner = dot(work[i * n : (i + 1) * n, :span], inverse[:span, :span], (1, 0))
-            inverse[i * n : (i + 1) * n, :span] = -dot(
-                inverse[i * n : (i + 1) * n, i * n : (i + 1) * n], inner, (1, 0)
-            )
+            diag_in = work[at, at]
+            if b:
+                before, done = slice((b - 1) * n, b * n), slice(0, b * n)
+                if b < chips - 1:
+                    lower_part = work[past, before]
+                    work[past, at] -= dot(lower_part, work[at, before], (1, 1))
+                    work[past, past] -= dot(lower_part, lower_part, (1, 1))
+                inner = dot(work[at, done], inverse[done, done], (1, 0))
+            if b == 2:
+                tied = couple_part(order[2], 0)
+                for k in range(1, fold // (2 * LANES)):
+                    tied = tied + couple_part(order[2], k)
+            diag = tile_inverse(diag_in)
+            inverse[at, at] = diag
+            if b == 2:
+                couple_send(2, tied)
+        with jax.named_scope("panel"):
+            if b < chips - 1:
+                scaled = dot(work[past, at], diag, (1, 1))
+                work[past, at] = scaled
+                work[(b + 1) * n : (b + 2) * n, (b + 1) * n : (b + 2) * n] -= dot(scaled[:n], scaled[:n], (1, 1))
+            if b:
+                inverse[at, done] = -dot(diag, inner, (1, 0))
+        between(b)
 
     with jax.named_scope("cross"):
         for k in range(chips):
@@ -1161,7 +1267,7 @@
 
 def final_kernel(gath_ref, rest_ref, weight_ref, out_ref, high, low):
     orbs, fold, n = gath_ref.shape
-    rows = out_ref.shape[1]
+    rows = out_ref.shape[1] * out_ref.shape[3]
     i = pl.program_id(0)
 
     @pl.when(i == 0)
@@ -1177,9 +1283,12 @@
         total = value if total is None else total + value
     lanes = lax.broadcasted_iota(jnp.int32, (rows, n), 1)
     kept = rest_ref[at, :]
+    count = out_ref.shape[1]
     for h in range(2):
         held = kept if h else pltpu.roll(kept, n // 2, 1)
-        out_ref[h] = jnp.where(lanes < n // 2, 0.0, held) + total[:, h * n : (h + 1) * n]
+        value = jnp.where(lanes < n // 2, 0.0, held) + total[:, h * n : (h + 1) * n]
+        for k in range(count):
+            out_ref[h, k, 0] = value[k * (rows // count) : (k + 1) * (rows // count)]
 
 
 def early_device(slabs, orbs, orbitals, potential):
@@ -1187,7 +1296,8 @@
     points = planes * rows_y * rows_z
     panel_dev = PANEL // orbs
     chips = orbs // 2
-    thin = points // LANES
+    slots = 2 * slabs
+    rows = points // slots
     fold = points // 2
     tiles = chips * (chips + 1) // 2
     block = tiles // 2 * LANES // slabs
@@ -1201,11 +1311,16 @@
             jax.ShapeDtypeStruct((fold, LANES), f32),
             jax.ShapeDtypeStruct((orbs * LANES, 2 * LANES), f32),
         ],
-        in_specs=[vmem] * 2,
+        in_specs=[pl.BlockSpec(memory_space=pltpu.HBM), vmem],
         out_specs=[vmem] * 3,
-        scratch_shapes=[pltpu.VMEM((slabs, points // slabs, LANES), f32)] * 4
+        scratch_shapes=[
+            pltpu.VMEM((slots, rows, LANES), f32),
+            pltpu.VMEM((LANES, LANES), f32),
+            pltpu.VMEM((rows_z, LANES), f32),
+        ]
+        + [pltpu.VMEM((slabs, points // slabs, LANES), f32)] * 4
         + [
-            pltpu.VMEM((slabs, thin, LANES), f32),
+            pltpu.VMEM((slabs, rows_z, LANES), f32),
             pltpu.VMEM((9 * points // 2, LANES), f32),
             pltpu.VMEM((9 * points // 2, LANES), f32),
             pltpu.VMEM((points // 2, LANES), f32),
@@ -1219,7 +1334,10 @@
             pltpu.VMEM((PANEL, PANEL), f32),
             pltpu.VMEM((PANEL, PANEL), f32),
         ]
-        + [dma((slabs,))] * 10
+        + [dma((2,))]
+        + [dma((4, slabs))] * 2
+        + [dma((slabs,))] * 2
+        + [dma((4, slabs))] * 2
         + [dma((2, orbs))] * 2
         + [dma((1,))]
         + [dma((orbs,))] * 2
@@ -1230,15 +1348,16 @@
         compiler_params=pltpu.CompilerParams(
             collective_id=0, has_side_effects=True, vmem_limit_bytes=40 << 20
         ),
-    )(orbitals.reshape(points, columns), potential.reshape(LANES, thin).T)
-    count = 4
+    )(orbitals.reshape(slots, rows, columns), potential.reshape(planes * rows_y, rows_z))
     whole = [pl.BlockSpec(memory_space=pltpu.VMEM)] * 3
     out = pl.pallas_call(
         final_kernel,
-        grid=(count,),
-        out_shape=jax.ShapeDtypeStruct((2, fold, LANES), f32),
+        grid=(slabs,),
+        out_shape=jax.ShapeDtypeStruct((2, slabs, 2, rows // 2, LANES), f32),
         in_specs=whole,
-        out_specs=pl.BlockSpec((2, fold // count, LANES), lambda i: (0, i, 0)),
+        out_specs=pl.BlockSpec(
+            (2, slabs // 2, 1, rows // 2, LANES), lambda i: (0, i % 2, i // 2, 0, 0)
+        ),
         scratch_shapes=[pltpu.VMEM((orbs * LANES, 2 * LANES), jnp.bfloat16)] * 2,
         compiler_params=pltpu.CompilerParams(vmem_limit_bytes=16 << 20),
     )(gath, rest, weight)
@@ -1256,7 +1375,7 @@
     dma = pltpu.SemaphoreType.DMA
     steps = max(orbs // 2 - 1, 1)
     split = folds == 2 and planes == slabs and rows_y // 2 >= REACH and steps >= 2
-    if split and orbs == 8 and PANEL == 4 * LANES and 5 * LANES % (8 * slabs) == 0:
+    if split and orbs == 8 and slabs == 4 and PANEL == 4 * LANES and planes * rows_y <= LANES:
         return early_device(slabs, orbs, orbitals, potential)
     flat = orbitals.reshape(points, columns)
     own, panel, gram, cross = pl.pallas_call(

time: 106 us -> 95.8 us (0.904)
  Pallas kernels: 103 us -> 93.6 us
    pallas_call x1, Pallas kernels: 100 us -> 90.2 us  [early_device(): pl.pallas_call(functools.partial(early_kernel, slabs, orbs, (planes, rows...]
where the time goes in v3:
time: 95.8 us; the launch traced here: 95.6 us
  Pallas kernels  93.6 us (98%)
  local copies, waits for them, and re-layouts  1.98 us (2%)
    pallas_call x1, Pallas kernels, early_device(): pl.pallas_call(functools.partial(early_kernel, slabs, orbs, (planes, rows...  90.2 us
    pallas_call x1, Pallas kernels, early_device(): pl.pallas_call(final_kernel, grid=(slabs,), out_shape=jax.ShapeDtypeStruc...  3.37 us
    unnamed x4, local copies, waits for them, and re-layouts  1.98 us

profile of v3, /device:TPU:0, one launch (start us, length us, event | category | flops | bytes accessed | tf_op | source)
XLA Modules:
  0.0 95.6 jit_solution(5746626310702627934)
XLA Ops:
  0.0 0.0 copy-start
  0.0 1.2 %copy-done = f32[4,16,32,128]{3,2,1,0:T(8,128)S(1)} copy-done((f32[4,16,32,128]{3,2,1,0:T(8,128)S(1)}, f32[4,16,32,128]{3,2,1,0:T(8,128)}, u32[]{:S(2)}) %copy-start) | copy-done | bytes 1048600
  1.2 0.0 copy-start.1
  1.2 0.8 copy-done.1
  2.0 90.2 %shard_map.28 = (f32[8,1024,128]{2,1,0:T(8,128)S(1)}, f32[1024,128]{1,0:T(8,128)S(1)}, f32[1024,256]{1,0:T(8,128)S(1)}) custom-call(f32[8,256,128]{2,1,0:T(8,128)S(1)} %bitcast.3, f32[64,32]{1,0:T(8,128)S(1)} %bitcast.4), custom_call_target="tpu_custom_call" | custom-call | tf_op jit(solution)/shard_map/pallas_call | solution.py:1307
  92.2 3.4 %shard_map.29 = f32[2,4,2,128,128]{4,3,2,1,0:T(8,128)} custom-call(f32[8,1024,128]{2,1,0:T(8,128)S(1)} %get-tuple-element.8.gath_ref, f32[1024,128]{1,0:T(8,128)S(1)} %get-tuple-element.9.rest_ref, f32[1024,256]{1,0:T(8,128)S(1)} %get-tuple-element.10.weight_ref), custom_call_target="tpu_custom_call" | custom-call | tf_op jit(solution)/shard_map/pallas_call | solution.py:1353
Async XLA Ops:
  0.0 1.2 %copy-start = (f32[4,16,32,128]{3,2,1,0:T(8,128)S(1)}, f32[4,16,32,128]{3,2,1,0:T(8,128)}, u32[]{:S(2)}) copy-start(f32[4,16,32,128]{3,2,1,0:T(8,128)} %param.2) | copy-start | bytes 3145732
  1.2 0.8 copy-start.1

commit v4 on v3

--- a/solution.py
+++ b/solution.py
@@ -766,7 +766,6 @@
     panel_dev = PANEL // orbs
     points_all = points * slabs
     step = 16
-    slot = lax.broadcasted_iota(jnp.int32, (step, LANES), 1) // width
 
     def fetch(c):
         view = slice(c * sub, (c + 1) * sub)
@@ -785,12 +784,17 @@
             barrier, inc=1, device_id={"orb": lax.rem(me + hop, orbs)}, device_id_type=MESH
         )
 
-    def merge(parts):
-        out = None
-        for u, (value, v) in enumerate(parts):
-            turn = ((u - v) * width) % LANES
-            value = pltpu.roll(value, turn, 1) if turn else value
-            out = value if out is None else jnp.where(slot == u, value, out)
+    def exchange_groups(x, unit):
+        lane = lax.broadcasted_iota(jnp.int32, (step, LANES), 1) // unit
+        outer, inner = lane // 2 % 2 == 0, lane % 2 == 0
+        pairs = [None] * 4
+        for a in range(2):
+            pairs[a] = jnp.where(outer, x[a], pltpu.roll(x[a + 2], 2 * unit, 1))
+            pairs[a + 2] = jnp.where(outer, pltpu.roll(x[a], LANES - 2 * unit, 1), x[a + 2])
+        out = [None] * 4
+        for a in (0, 2):
+            out[a] = jnp.where(inner, pairs[a], pltpu.roll(pairs[a + 1], unit, 1))
+            out[a + 1] = jnp.where(inner, pltpu.roll(pairs[a], LANES - unit, 1), pairs[a + 1])
         return out
 
     def over(c, body):
@@ -798,7 +802,7 @@
             body(pl.multiple_of(c * sub + block * step, step))
             return carry
 
-        lax.fori_loop(0, sub // step, one, 0)
+        lax.fori_loop(0, sub // step, one, 0, unroll=2)
 
     def span(h, c):
         return slice(h * rows + c * sub, h * rows + (c + 1) * sub)
@@ -821,16 +825,22 @@
     def pack_part(h, c):
         def body(at):
             parts = [x_ref[q, pl.ds(at, step), :] for q in range(slots)]
-            for j in range(slabs):
-                pack[j, pl.ds(h * rows + at, step), :] = merge([(part, h * slabs + j) for part in parts])
+            lane = lax.broadcasted_iota(jnp.int32, (step, LANES), 1)
+            turned = [pltpu.roll(part, LANES // 2, 1) for part in (parts[:slabs] if h else parts[slabs:])]
+            joined = [
+                jnp.where(lane < LANES // 2, turned[u] if h else parts[u], parts[u + slabs] if h else turned[u])
+                for u in range(slabs)
+            ]
+            for j, value in enumerate(exchange_groups(joined, width)):
+                pack[j, pl.ds(h * rows + at, step), :] = value
 
         with jax.named_scope("pack"):
             over(c, body)
 
     def put(target, p, row, value):
-        odd = lax.rem(lax.broadcasted_iota(jnp.int32, value.shape, 1) // width, 2)
+        lane = lax.broadcasted_iota(jnp.int32, value.shape, 1)
         size = value.shape[0]
-        swapped = jnp.where(odd == 0, pltpu.roll(value, LANES - width, 1), pltpu.roll(value, width, 1))
+        swapped = jnp.take_along_axis(value, jnp.where(lane // width % 2 == 0, lane + width, lane - width), axis=1)
         target[pl.ds((planes + p) * plane + rows + row, size), :] = value
         target[pl.ds((planes + p) * plane + row, size), :] = swapped
         target[pl.ds((planes + p) * plane + 2 * rows + row, size), :] = swapped
@@ -858,26 +868,23 @@
                 put(target, p, row, total)
             return carry
 
-        lax.fori_loop(low, high, body, 0)
-
-    def filter_half(h, during, ready):
+        lax.fori_loop(low, high, body, 0, unroll=rows_y // 4)
+
+    def filter_half(h, ready):
         for c in range(2):
             with jax.named_scope("wait_a"):
                 wait(pack, land, h, c, out_sems)
 
             def unpack(at):
                 parts = [land[i, pl.ds(h * rows + at, step), :] for i in range(slabs)]
-                for p in range(planes):
-                    put(wide_a, p, at, merge([(parts[u // 2], 2 * p + u % 2) for u in range(slots)]))
+                for p, value in enumerate(exchange_groups(parts, 2 * width)):
+                    put(wide_a, p, at, value)
 
             with jax.named_scope("unpack"):
                 over(c, unpack)
-        during[0]()
         source, target = wide_a, wide_b
         with jax.named_scope("sweep"):
             for order in range(DEGREE - 1):
-                if order == 2:
-                    during[1]()
                 sweep(source, target, order == 0)
                 source, target = target, source
         for c in range(2):
@@ -886,10 +893,8 @@
 
             def body(at):
                 parts = [target[pl.ds((planes + p) * plane + rows + at, step), :] for p in range(planes)]
-                for i in range(slabs):
-                    pack_back[i, pl.ds(h * rows + at, step), :] = merge(
-                        [(parts[q // 2], 2 * i + q % 2) for q in range(slots)]
-                    )
+                for i, value in enumerate(exchange_groups(parts, 2 * width)):
+                    pack_back[i, pl.ds(h * rows + at, step), :] = value
 
             with jax.named_scope("pack_b"):
                 over(c, body)
@@ -901,12 +906,9 @@
 
         def body(at):
             parts = [land_back[j, pl.ds(h * rows + at, step), :] for j in range(slabs)]
-            for k in range(slabs):
+            for k, value in enumerate(exchange_groups(parts, width)):
                 row = pl.multiple_of(c * part_rows + k * sub + at - c * sub, step)
-                store(
-                    pl.ds(row, step),
-                    merge([(parts[u % slabs], (u // slabs) * slabs + k) for u in range(slots)]),
-                )
+                store(pl.ds(row, step), value)
 
         with jax.named_scope("fold"):
             over(c, body)
@@ -928,15 +930,20 @@
     pot_land[here] = pot_mine[...]
     with jax.named_scope("level"):
         wait_exchange(slabs, here, p_send, p_recv, lambda there: pot_mine, pot_land)
-        lane_slot = lax.broadcasted_iota(jnp.int32, (rows_z, LANES), 1) // width
-        fields = [pot_land[s] for s in range(slabs)]
+        lane = lax.broadcasted_iota(jnp.int32, (rows_z, LANES), 1)
+        lane_slot = lane // width
+        held = LANES // 2
+        fields = [
+            jnp.where(lane < held, pot_land[2 * s], pltpu.roll(pot_land[2 * s + 1], held, 1))
+            for s in range(slabs // 2)
+        ]
+        first = lane_slot // 2 % 2 * held + lane_slot % 2 * (rows_y // 2)
         for p in range(planes):
             for y in range(rows_y // 2):
-                value = None
-                for u in range(slots):
-                    l = p * rows_y + u % 2 * (rows_y // 2) + y
-                    spread = jnp.broadcast_to(fields[u // 2][:, l : l + 1], (rows_z, LANES))
-                    value = spread if value is None else jnp.where(lane_slot == u, spread, value)
+                taken = [
+                    jnp.take_along_axis(field, first + (p * rows_y + y), axis=1) for field in fields
+                ]
+                value = jnp.where(lane < held, taken[0], taken[1])
                 level[pl.ds(p * rows + y * rows_z, rows_z), :] = (
                     value - (SHIFT_MID + 1.5 * STENCIL[0])
                 ) * (1.0 / HALF_WIDTH)
@@ -1014,21 +1021,26 @@
     def settle_own():
         by_chip(own_items, lambda way, o, h: across(o, h, 1 - core).wait_recv())
 
-    def drain():
-        for z in (0, chips - 1):
-            on_chip(z, lambda: direct(z).wait_send())
-        for table in starts + passed:
-            by_chip(table, lambda *item: along(*item).wait_send())
-        for table in [own_items] + arrive:
-            by_chip(table, lambda way, o, h: across(o, h, core).wait_send())
-
-    def send_trailing():
-        for c in range(2):
-            send(pack, land, 1, c, out_sems)
-
-    filter_half(
-        0, (send_trailing, lambda: None), lambda c: send(pack_back, land_back, 0, c, back_sems)
-    )
+    def drain(first, past):
+        for z in range(chips):
+            def run():
+                if first == 0 and z in (0, chips - 1):
+                    direct(z).wait_send()
+                sent = (starts if first == 0 else []) + passed[first:past]
+                for table in sent:
+                    for item in table.get(z, []):
+                        along(*item).wait_send()
+                for h in range(2 if first == 0 else 0):
+                    across(z, h, core).wait_send()
+                for table in arrive[first:past]:
+                    for way, o, h in table.get(z, []):
+                        across(o, h, core).wait_send()
+
+            on_chip(z, run)
+
+    for c in range(2):
+        send(pack, land, 1, c, out_sems)
+    filter_half(0, lambda c: send(pack_back, land_back, 0, c, back_sems))
 
     def store_panel(at, value):
         gath[me, at, :] = value
@@ -1037,11 +1049,9 @@
         fold_part(0, c, store_panel)
         begin(c)
 
-    def early():
-        receive(0)
-        forward(0)
-
-    filter_half(1, (lambda: None, early), lambda c: None)
+    filter_half(1, lambda c: send(pack_back, land_back, 1, c, back_sems))
+    receive(0)
+    forward(0)
     receive(1)
     forward(1)
     settle_own()
@@ -1050,11 +1060,14 @@
 
     tiles = chips * (chips + 1) // 2
     share = tiles // 2
+    duties = [[(3, (0, 1, 2, 3)), (0, (0,))], [(2, (0, 1, 2)), (1, (0, 1))]]
     block = share * LANES // slabs
     centre = (chip + 1) // 2 == 1
 
-    def block_at(s):
-        return pl.ds(pl.multiple_of(s * block, 8), block)
+    piece = block // 2
+
+    def block_at(s, g):
+        return pl.ds(pl.multiple_of(s * block + g * piece, 8), piece)
 
     def pair(z, at):
         return jnp.concatenate([gath[z * 2, at, :], gath[z * 2 + 1, at, :]], axis=1)
@@ -1063,91 +1076,95 @@
     def _():
         at = pl.ds(pl.multiple_of((chip - 1) * part_rows, part_rows), part_rows)
 
-        def tile(n, carry):
-            t = core * share + n
-            za = (t + 8) // 9 + (t + 6) // 9 + (t + 3) // 9
-            zb = t - za * (za + 1) // 2
-            product = dot_pieces(pieces(pair(za, at)), pieces(pair(zb, at)), (0, 0))
-            for r, value in enumerate(unfolded(product, 2)):
-                gram_part[pl.ds(pl.multiple_of(n * LANES + r * panel_dev, panel_dev), panel_dev), :] = value
-            return carry
-
         with jax.named_scope("gram"):
-            lax.fori_loop(0, share, tile, 0)
-        exchange(slabs, here, r_send, r_recv, lambda there: gram_part.at[block_at(there)], gram_land)
-
-    for c in range(2):
-        send(pack_back, land_back, 1, c, back_sems)
-
-    def spread(index, there):
-        view = gram_chip.at[index]
+            for c, groups in enumerate(duties):
+                def run():
+                    n = 0
+                    for za, zbs in groups:
+                        left = pieces(pair(za, at).T)
+                        for zb in zbs:
+                            product = dot_pieces(left, pieces(pair(zb, at)), (1, 0))
+                            for r, value in enumerate(unfolded(product, 2)):
+                                gram_part[n * LANES + r * panel_dev : n * LANES + (r + 1) * panel_dev, :] = value
+                            n += 1
+
+                pl.when(core == c)(run)
+        for g in range(2):
+            exchange(
+                slabs, here, r_send.at[g], r_recv.at[g],
+                lambda there: gram_part.at[block_at(there, g)], gram_land.at[g],
+            )
+
+    def spread(g, index, there):
+        view = gram_chip.at[g, index]
         return pltpu.make_async_remote_copy(
             src_ref=view,
             dst_ref=view,
-            send_sem=z_send.at[there],
-            recv_sem=z_recv.at[index],
+            send_sem=z_send.at[g, there],
+            recv_sem=z_recv.at[g, index],
             device_id={"orb": there * 2 + core},
             device_id_type=MESH,
         )
 
-    @pl.when(centre)
-    def _():
-        with jax.named_scope("wait_r"):
-            wait_exchange(slabs, here, r_send, r_recv, lambda there: gram_part.at[block_at(there)], gram_land)
-        gram_land[here] = gram_part[block_at(here), :]
-        total = gram_land[0]
-        for s in range(1, slabs):
-            total += gram_land[s]
-        gram_chip[chip - 1] = total / points_all
-
-    for z in range(1, 3):
-        def body():
-            for there in range(chips):
-                if there != z:
-                    spread(z - 1, there).start()
-
-        on_chip(z, body)
+    for g in range(2):
+        @pl.when(centre)
+        def _():
+            with jax.named_scope("wait_r"):
+                wait_exchange(
+                    slabs, here, r_send.at[g], r_recv.at[g],
+                    lambda there: gram_part.at[block_at(there, g)], gram_land.at[g],
+                )
+            gram_land[g, here] = gram_part[block_at(here, g), :]
+            total = gram_land[g, 0]
+            for s in range(1, slabs):
+                total += gram_land[g, s]
+            gram_chip[g, chip - 1] = total / points_all
+
+        for z in range(1, 3):
+            def body():
+                for there in range(chips):
+                    if there != z:
+                        spread(g, z - 1, there).start()
+
+            on_chip(z, body)
     forward(2)
-
-    with jax.named_scope("wait_z"):
-        for z in range(chips):
-            def body():
-                for index in range(2):
-                    if z != index + 1:
-                        spread(index, z).wait_recv()
-                    else:
-                        for there in range(chips):
-                            if there != z:
-                                spread(index, there).wait_send()
-
-            on_chip(z, body)
-    gram_all[core, block_at(here), :] = gram_chip[0] + gram_chip[1]
-
-    def gram_side(side, s):
-        view = gram_all.at[side, block_at(s)]
+    weight_ref[...] = jnp.zeros_like(weight_ref)
+
+    def gram_side(g, side, s):
+        view = gram_all.at[side, block_at(s, g)]
         return pltpu.make_async_remote_copy(
             src_ref=view,
             dst_ref=view,
-            send_sem=t_send.at[s],
-            recv_sem=t_recv.at[s],
+            send_sem=t_send.at[g, s],
+            recv_sem=t_recv.at[g, s],
             device_id={"orb": partner},
             device_id_type=MESH,
         )
 
-    def plane_copy(hop, s, there):
-        view = gram_all.at[core, block_at(s)]
+    def plane_copy(g, hop, s, there):
+        view = gram_all.at[core, block_at(s, g)]
         return pltpu.make_async_remote_copy(
             src_ref=view,
             dst_ref=view,
-            send_sem=s_send.at[hop],
-            recv_sem=s_recv.at[hop],
+            send_sem=s_send.at[g, hop],
+            recv_sem=s_recv.at[g, hop],
             device_id={"space": there},
             device_id_type=MESH,
         )
 
-    for hop in range(1, slabs):
-        plane_copy(hop, here, lax.rem(here + hop, slabs)).start()
-    gram_side(core, here).start()
+    for g in range(2):
+        with jax.named_scope("wait_z"):
+            for z in range(chips):
+                def body():
+                    for index in range(2):
+                        if z != index + 1:
+                            spread(g, index, z).wait_recv()
+
+                on_chip(z, body)
+        gram_all[core, block_at(here, g), :] = gram_chip[g, 0] + gram_chip[g, 1]
+        for hop in range(1, slabs):
+            plane_copy(g, hop, here, lax.rem(here + hop, slabs)).start()
+        gram_side(g, core, here).start()
 
     def store_rest(at, value):
         rest_ref[at, :] = value
@@ -1177,31 +1194,38 @@
     order = [chip, chip + 1 - 2 * lax.rem(chip, 2), 2 - lower, 3 - 3 * lower]
     receive(2)
     forward(3)
+    with jax.named_scope("drain"):
+        drain(0, 3)
+        for z in range(1, 3):
+            def body():
+                for g in range(2):
+                    for there in range(chips):
+                        if there != z:
+                            spread(g, z - 1, there).wait_send()
+
+            on_chip(z, body)
     with jax.named_scope("wait_s"):
-        for hop in range(1, slabs):
-            source = lax.rem(here + slabs - hop, slabs)
-            plane_copy(hop, source, lax.rem(here + hop, slabs)).wait_recv()
-            gram_side(core, source).start()
-    couple(0, order[0])
+        for g in range(2):
+            for hop in range(1, slabs):
+                source = lax.rem(here + slabs - hop, slabs)
+                plane_copy(g, hop, source, lax.rem(here + hop, slabs)).wait_recv()
+                gram_side(g, core, source).start()
     settle(2)
-    receive(3)
-    forward(4)
-    couple(1, order[1])
     with jax.named_scope("wait_t"):
-        for s in range(slabs):
-            gram_side(1 - core, s).wait_recv()
+        for g in range(2):
+            for s in range(slabs):
+                gram_side(g, 1 - core, s).wait_recv()
 
     n = LANES
     inverse[...] = jnp.zeros_like(inverse)
-    for za in range(chips):
-        for zb in range(za + 1):
-            t = za * (za + 1) // 2 + zb
-            work[za * n : (za + 1) * n, zb * n : (zb + 1) * n] = gram_all[
-                t // share, (t % share) * n : (t % share + 1) * n, :
-            ]
+    for c, groups in enumerate(duties):
+        for k, (za, zb) in enumerate([(za, zb) for za, zbs in groups for zb in zbs]):
+            work[za * n : (za + 1) * n, zb * n : (zb + 1) * n] = gram_all[c, k * n : (k + 1) * n, :]
 
     def between(b):
         if b == 0:
+            receive(3)
+            forward(4)
             receive(4)
         if b == 1:
             settle(3)
@@ -1222,14 +1246,14 @@
                     work[past, at] -= dot(lower_part, work[at, before], (1, 1))
                     work[past, past] -= dot(lower_part, lower_part, (1, 1))
                 inner = dot(work[at, done], inverse[done, done], (1, 0))
-            if b == 2:
-                tied = couple_part(order[2], 0)
-                for k in range(1, fold // (2 * LANES)):
-                    tied = tied + couple_part(order[2], k)
+            tied = None
+            for k in range(fold // (2 * LANES) if b < chips - 1 else 0):
+                term = couple_part(order[b], k)
+                tied = term if tied is None else tied + term
             diag = tile_inverse(diag_in)
             inverse[at, at] = diag
-            if b == 2:
-                couple_send(2, tied)
+            if b < chips - 1:
+                couple_send(b, tied)
         with jax.named_scope("panel"):
             if b < chips - 1:
                 scaled = dot(work[past, at], diag, (1, 1))
@@ -1249,20 +1273,22 @@
                 total += cross_land[k, s]
             cross[:, pl.ds(pl.multiple_of(order[k] * LANES, LANES), LANES)] = total / points_all
     with jax.named_scope("weights"):
-        middle = dot(cross[...], inverse[...], (1, 1))
-        trail = -dot(middle, inverse[...], (1, 0))
+        factors = pieces(inverse[...])
+        middle = dot_pieces(pieces(cross[...]), factors, (1, 1))
+        trail = -dot_pieces(pieces(middle), factors, (1, 0))
         own = inverse[pl.ds(pl.multiple_of(me * panel_dev, panel_dev), panel_dev), :]
         turned = jnp.concatenate([own, trail], axis=0).T
-        weight_ref[...] = jnp.zeros_like(weight_ref)
         for o in range(orbs):
             value = turned[o * panel_dev : (o + 1) * panel_dev]
             weight_ref[o * LANES : o * LANES + panel_dev, :LANES] = value
             weight_ref[o * LANES + panel_dev : (o + 1) * LANES, LANES:] = value
-    drain()
-    for hop in range(1, slabs):
-        plane_copy(hop, here, lax.rem(here + hop, slabs)).wait_send()
-    for s in range(slabs):
-        gram_side(core, s).wait_send()
+    with jax.named_scope("last"):
+        drain(3, 6)
+    for g in range(2):
+        for hop in range(1, slabs):
+            plane_copy(g, hop, here, lax.rem(here + hop, slabs)).wait_send()
+        for s in range(slabs):
+            gram_side(g, core, s).wait_send()
 
 
 def final_kernel(gath_ref, rest_ref, weight_ref, out_ref, high, low):
@@ -1325,8 +1351,8 @@
             pltpu.VMEM((9 * points // 2, LANES), f32),
             pltpu.VMEM((points // 2, LANES), f32),
             pltpu.VMEM((slabs * block, LANES), f32),
-            pltpu.VMEM((slabs, block, LANES), f32),
-            pltpu.VMEM((2, block, LANES), f32),
+            pltpu.VMEM((2, slabs, block // 2, LANES), f32),
+            pltpu.VMEM((2, 2, block // 2, LANES), f32),
             pltpu.VMEM((2, slabs * block, LANES), f32),
             pltpu.VMEM((chips, panel_dev, LANES), f32),
             pltpu.VMEM((chips, slabs, panel_dev, LANES), f32),
@@ -1341,9 +1367,9 @@
         + [dma((2, orbs))] * 2
         + [dma((1,))]
         + [dma((orbs,))] * 2
-        + [dma((slabs,))] * 2
-        + [dma((chips,)), dma((2,))]
-        + [dma((slabs,))] * 4
+        + [dma((2, slabs))] * 2
+        + [dma((2, chips)), dma((2, 2))]
+        + [dma((2, slabs))] * 4
         + [dma((chips, slabs))] * 2,
         compiler_params=pltpu.CompilerParams(
             collective_id=0, has_side_effects=True, vmem_limit_bytes=40 << 20
@@ -1375,7 +1401,7 @@
     dma = pltpu.SemaphoreType.DMA
     steps = max(orbs // 2 - 1, 1)
     split = folds == 2 and planes == slabs and rows_y // 2 >= REACH and steps >= 2
-    if split and orbs == 8 and slabs == 4 and PANEL == 4 * LANES and planes * rows_y <= LANES:
+    if split and orbs == 8 and slabs == 4 and PANEL == 4 * LANES and 2 * planes * rows_y == LANES:
         return early_device(slabs, orbs, orbitals, potential)
     flat = orbitals.reshape(points, columns)
     own, panel, gram, cross = pl.pallas_call(

time: 95.8 us -> 83.8 us (0.87)
  Pallas kernels: 93.6 us -> 81.6 us
    pallas_call x1, Pallas kernels: 90.2 us -> 78.3 us  [early_device(): pl.pallas_call(functools.partial(early_kernel, slabs, orbs, (planes, rows...]
where the time goes in v4:
time: 83.8 us; the launch traced here: 83.6 us
  Pallas kernels  81.6 us (97%)
  local copies, waits for them, and re-layouts  1.98 us (2%)
    pallas_call x1, Pallas kernels, early_device(): pl.pallas_call(functools.partial(early_kernel, slabs, orbs, (planes, rows...  78.3 us
    pallas_call x1, Pallas kernels, early_device(): pl.pallas_call(final_kernel, grid=(slabs,), out_shape=jax.ShapeDtypeStruc...  3.37 us
    unnamed x4, local copies, waits for them, and re-layouts  1.98 us

profile of v4, /device:TPU:0, one launch (start us, length us, event | category | flops | bytes accessed | tf_op | source)
XLA Modules:
  0.0 83.6 jit_solution(11076180150548618310)
XLA Ops:
  0.0 0.0 copy-start
  0.0 1.2 %copy-done = f32[4,16,32,128]{3,2,1,0:T(8,128)S(1)} copy-done((f32[4,16,32,128]{3,2,1,0:T(8,128)S(1)}, f32[4,16,32,128]{3,2,1,0:T(8,128)}, u32[]{:S(2)}) %copy-start) | copy-done | bytes 1048600
  1.2 0.0 copy-start.1
  1.2 0.8 copy-done.1
  2.0 78.3 %shard_map.28 = (f32[8,1024,128]{2,1,0:T(8,128)S(1)}, f32[1024,128]{1,0:T(8,128)S(1)}, f32[1024,256]{1,0:T(8,128)S(1)}) custom-call(f32[8,256,128]{2,1,0:T(8,128)S(1)} %bitcast.3, f32[64,32]{1,0:T(8,128)S(1)} %bitcast.4), custom_call_target="tpu_custom_call" | custom-call | tf_op jit(solution)/shard_map/pallas_call | solution.py:1333
  80.3 3.4 %shard_map.29 = f32[2,4,2,128,128]{4,3,2,1,0:T(8,128)} custom-call(f32[8,1024,128]{2,1,0:T(8,128)S(1)} %get-tuple-element.8.gath_ref, f32[1024,128]{1,0:T(8,128)S(1)} %get-tuple-element.9.rest_ref, f32[1024,256]{1,0:T(8,128)S(1)} %get-tuple-element.10.weight_ref), custom_call_target="tpu_custom_call" | custom-call | tf_op jit(solution)/shard_map/pallas_call | solution.py:1379
Async XLA Ops:
  0.0 1.2 %copy-start = (f32[4,16,32,128]{3,2,1,0:T(8,128)S(1)}, f32[4,16,32,128]{3,2,1,0:T(8,128)}, u32[]{:S(2)}) copy-start(f32[4,16,32,128]{3,2,1,0:T(8,128)} %param.2) | copy-start | bytes 3145732
  1.2 0.8 copy-start.1

commit v5 on v4

--- a/solution.py
+++ b/solution.py
@@ -52,8 +52,8 @@
         copy = pltpu.make_async_remote_copy(
             src_ref=send(there),
             dst_ref=land.at[here],
-            send_sem=send_sem.at[hop],
-            recv_sem=recv_sem.at[hop],
+            send_sem=send_sem.at[hop - 1],
+            recv_sem=recv_sem.at[hop - 1],
             device_id={"space": there},
             device_id_type=MESH,
         )
@@ -69,8 +69,8 @@
         pltpu.make_async_remote_copy(
             src_ref=send(there),
             dst_ref=land.at[source],
-            send_sem=send_sem.at[hop],
-            recv_sem=recv_sem.at[hop],
+            send_sem=send_sem.at[hop - 1],
+            recv_sem=recv_sem.at[hop - 1],
             device_id={"space": there},
             device_id_type=MESH,
         ).wait()
@@ -916,15 +916,14 @@
     pot_wide[...] = jnp.zeros_like(pot_wide)
     pot_wide[: planes * rows_y, :rows_z] = pot_ref[...]
     pot_mine[...] = pot_wide[...].T[:rows_z]
-    fetch(0).wait()
-    pack_part(0, 0)
+    for c in range(2):
+        fetch(c).wait()
+        pack_part(0, c)
     with jax.named_scope("barrier"):
         pl.semaphore_wait(barrier, slabs - 1 + orbs - 1)
     exchange(slabs, here, p_send, p_recv, lambda there: pot_mine, pot_land)
-    send(pack, land, 0, 0, out_sems)
-    fetch(1).wait()
-    pack_part(0, 1)
-    send(pack, land, 0, 1, out_sems)
+    for c in range(2):
+        send(pack, land, 0, c, out_sems)
     for c in range(2):
         pack_part(1, c)
     pot_land[here] = pot_mine[...]
@@ -956,7 +955,7 @@
             src_ref=view,
             dst_ref=view,
             send_sem=along_send.at[way, origin * 2 + h],
-            recv_sem=along_recv.at[way, origin * 2 + h],
+            recv_sem=along_recv.at[origin * 2 + h],
             device_id={"orb": (chip + 1 - 2 * way) * 2 + core},
             device_id_type=MESH,
         )
@@ -968,7 +967,7 @@
             src_ref=view,
             dst_ref=view,
             send_sem=direct_send.at[0],
-            recv_sem=along_recv.at[way, z * 2 + h],
+            recv_sem=along_recv.at[z * 2 + h],
             device_id={"orb": (z + 2 - 4 * way) * 2 + core},
             device_id_type=MESH,
         )
@@ -1049,7 +1048,7 @@
         fold_part(0, c, store_panel)
         begin(c)
 
-    filter_half(1, lambda c: send(pack_back, land_back, 1, c, back_sems))
+    filter_half(1, lambda c: None)
     receive(0)
     forward(0)
     receive(1)
@@ -1094,6 +1093,9 @@
                 slabs, here, r_send.at[g], r_recv.at[g],
                 lambda there: gram_part.at[block_at(there, g)], gram_land.at[g],
             )
+
+    for c in range(2):
+        send(pack_back, land_back, 1, c, back_sems)
 
     def spread(g, index, there):
         view = gram_chip.at[g, index]
@@ -1129,6 +1131,8 @@
             on_chip(z, body)
     forward(2)
     weight_ref[...] = jnp.zeros_like(weight_ref)
+    with jax.named_scope("drain"):
+        drain(0, 2)
 
     def gram_side(g, side, s):
         view = gram_all.at[side, block_at(s, g)]
@@ -1146,8 +1150,8 @@
         return pltpu.make_async_remote_copy(
             src_ref=view,
             dst_ref=view,
-            send_sem=s_send.at[g, hop],
-            recv_sem=s_recv.at[g, hop],
+            send_sem=s_send.at[g, hop - 1],
+            recv_sem=s_recv.at[g, hop - 1],
             device_id={"space": there},
             device_id_type=MESH,
         )
@@ -1184,33 +1188,21 @@
 
     def couple(n, z):
         with jax.named_scope("couple"):
-            total = lax.fori_loop(
-                0, fold // (2 * LANES), lambda k, total: total + couple_part(z, k),
-                jnp.zeros((LANES, 2 * LANES), jnp.float32),
-            )
+            total = couple_part(z, 0)
+            for k in range(1, fold // (2 * LANES)):
+                total += couple_part(z, k)
         couple_send(n, total)
 
     lower = chip // 2
     order = [chip, chip + 1 - 2 * lax.rem(chip, 2), 2 - lower, 3 - 3 * lower]
     receive(2)
     forward(3)
-    with jax.named_scope("drain"):
-        drain(0, 3)
-        for z in range(1, 3):
-            def body():
-                for g in range(2):
-                    for there in range(chips):
-                        if there != z:
-                            spread(g, z - 1, there).wait_send()
-
-            on_chip(z, body)
     with jax.named_scope("wait_s"):
         for g in range(2):
             for hop in range(1, slabs):
                 source = lax.rem(here + slabs - hop, slabs)
                 plane_copy(g, hop, source, lax.rem(here + hop, slabs)).wait_recv()
                 gram_side(g, core, source).start()
-    settle(2)
     with jax.named_scope("wait_t"):
         for g in range(2):
             for s in range(slabs):
@@ -1224,6 +1216,7 @@
 
     def between(b):
         if b == 0:
+            settle(2)
             receive(3)
             forward(4)
             receive(4)
@@ -1283,7 +1276,15 @@
             weight_ref[o * LANES : o * LANES + panel_dev, :LANES] = value
             weight_ref[o * LANES + panel_dev : (o + 1) * LANES, LANES:] = value
     with jax.named_scope("last"):
-        drain(3, 6)
+        drain(2, 6)
+        for z in range(1, 3):
+            def body():
+                for g in range(2):
+                    for there in range(chips):
+                        if there != z:
+                            spread(g, z - 1, there).wait_send()
+
+            on_chip(z, body)
     for g in range(2):
         for hop in range(1, slabs):
             plane_copy(g, hop, here, lax.rem(here + hop, slabs)).wait_send()
@@ -1361,16 +1362,16 @@
             pltpu.VMEM((PANEL, PANEL), f32),
         ]
         + [dma((2,))]
-        + [dma((4, slabs))] * 2
-        + [dma((slabs,))] * 2
-        + [dma((4, slabs))] * 2
-        + [dma((2, orbs))] * 2
-        + [dma((1,))]
+        + [dma((4, slabs - 1))] * 2
+        + [dma((slabs - 1,))] * 2
+        + [dma((4, slabs - 1))] * 2
+        + [dma((2, orbs)), dma((orbs,)), dma((1,))]
         + [dma((orbs,))] * 2
+        + [dma((2, slabs - 1))] * 2
+        + [dma((2, chips)), dma((2, 2))]
+        + [dma((2, slabs - 1))] * 2
         + [dma((2, slabs))] * 2
-        + [dma((2, chips)), dma((2, 2))]
-        + [dma((2, slabs))] * 4
-        + [dma((chips, slabs))] * 2,
+        + [dma((chips, slabs - 1))] * 2,
         compiler_params=pltpu.CompilerParams(
             collective_id=0, has_side_effects=True, vmem_limit_bytes=40 << 20
         ),

time: 83.8 us -> 82.8 us (0.988)
  Pallas kernels: 81.6 us -> 80.6 us
    pallas_call x1, Pallas kernels: 78.3 us -> 77.2 us  [early_device(): pl.pallas_call(functools.partial(early_kernel, slabs, orbs, (planes, rows...]
where the time goes in v5:
time: 82.8 us; the launch traced here: 82.6 us
  Pallas kernels  80.6 us (97%)
  local copies, waits for them, and re-layouts  1.98 us (2%)
    pallas_call x1, Pallas kernels, early_device(): pl.pallas_call(functools.partial(early_kernel, slabs, orbs, (planes, rows...  77.2 us
    pallas_call x1, Pallas kernels, early_device(): pl.pallas_call(final_kernel, grid=(slabs,), out_shape=jax.ShapeDtypeStruc...  3.37 us
    unnamed x4, local copies, waits for them, and re-layouts  1.98 us

profile of v5, /device:TPU:0, one launch (start us, length us, event | category | flops | bytes accessed | tf_op | source)
XLA Modules:
  0.0 82.6 jit_solution(8054205112856458083)
XLA Ops:
  0.0 0.0 copy-start
  0.0 1.2 %copy-done = f32[4,16,32,128]{3,2,1,0:T(8,128)S(1)} copy-done((f32[4,16,32,128]{3,2,1,0:T(8,128)S(1)}, f32[4,16,32,128]{3,2,1,0:T(8,128)}, u32[]{:S(2)}) %copy-start) | copy-done | bytes 1048600
  1.2 0.0 copy-start.1
  1.2 0.8 copy-done.1
  2.0 77.2 %shard_map.28 = (f32[8,1024,128]{2,1,0:T(8,128)S(1)}, f32[1024,128]{1,0:T(8,128)S(1)}, f32[1024,256]{1,0:T(8,128)S(1)}) custom-call(f32[8,256,128]{2,1,0:T(8,128)S(1)} %bitcast.3, f32[64,32]{1,0:T(8,128)S(1)} %bitcast.4), custom_call_target="tpu_custom_call" | custom-call | tf_op jit(solution)/shard_map/pallas_call | solution.py:1334
  79.2 3.4 %shard_map.29 = f32[2,4,2,128,128]{4,3,2,1,0:T(8,128)} custom-call(f32[8,1024,128]{2,1,0:T(8,128)S(1)} %get-tuple-element.8.gath_ref, f32[1024,128]{1,0:T(8,128)S(1)} %get-tuple-element.9.rest_ref, f32[1024,256]{1,0:T(8,128)S(1)} %get-tuple-element.10.weight_ref), custom_call_target="tpu_custom_call" | custom-call | tf_op jit(solution)/shard_map/pallas_call | solution.py:1380
Async XLA Ops:
  0.0 1.2 %copy-start = (f32[4,16,32,128]{3,2,1,0:T(8,128)S(1)}, f32[4,16,32,128]{3,2,1,0:T(8,128)}, u32[]{:S(2)}) copy-start(f32[4,16,32,128]{3,2,1,0:T(8,128)} %param.2) | copy-start | bytes 3145732
  1.2 0.8 copy-start.1

commit v6 on v5

--- a/solution.py
+++ b/solution.py
@@ -1173,8 +1173,6 @@
     def store_rest(at, value):
         rest_ref[at, :] = value
 
-    for c in range(2):
-        fold_part(1, c, store_rest)
 
     def couple_part(z, k):
         at = pl.ds(pl.multiple_of(k * 2 * LANES, 2 * LANES), 2 * LANES)
@@ -1203,6 +1201,8 @@
                 source = lax.rem(here + slabs - hop, slabs)
                 plane_copy(g, hop, source, lax.rem(here + hop, slabs)).wait_recv()
                 gram_side(g, core, source).start()
+    for c in range(2):
+        fold_part(1, c, store_rest)
     with jax.named_scope("wait_t"):
         for g in range(2):
             for s in range(slabs):

time: 82.8 us -> 83.4 us (level)
  no operation moved by 1% of the time
where the time goes in v6:
time: 83.4 us; the launch traced here: 83.2 us
  Pallas kernels  81.2 us (97%)
  local copies, waits for them, and re-layouts  1.98 us (2%)
    pallas_call x1, Pallas kernels, early_device(): pl.pallas_call(functools.partial(early_kernel, slabs, orbs, (planes, rows...  77.8 us
    pallas_call x1, Pallas kernels, early_device(): pl.pallas_call(final_kernel, grid=(slabs,), out_shape=jax.ShapeDtypeStruc...  3.37 us
    unnamed x4, local copies, waits for them, and re-layouts  1.98 us

profile of v6, /device:TPU:0, one launch (start us, length us, event | category | flops | bytes accessed | tf_op | source)
XLA Modules:
  0.0 83.2 jit_solution(12167967717200094240)
XLA Ops:
  0.0 0.0 copy-start
  0.0 1.2 %copy-done = f32[4,16,32,128]{3,2,1,0:T(8,128)S(1)} copy-done((f32[4,16,32,128]{3,2,1,0:T(8,128)S(1)}, f32[4,16,32,128]{3,2,1,0:T(8,128)}, u32[]{:S(2)}) %copy-start) | copy-done | bytes 1048600
  1.2 0.0 copy-start.1
  1.2 0.8 copy-done.1
  2.0 77.8 %shard_map.28 = (f32[8,1024,128]{2,1,0:T(8,128)S(1)}, f32[1024,128]{1,0:T(8,128)S(1)}, f32[1024,256]{1,0:T(8,128)S(1)}) custom-call(f32[8,256,128]{2,1,0:T(8,128)S(1)} %bitcast.3, f32[64,32]{1,0:T(8,128)S(1)} %bitcast.4), custom_call_target="tpu_custom_call" | custom-call | tf_op jit(solution)/shard_map/pallas_call | solution.py:1334
  79.8 3.4 %shard_map.29 = f32[2,4,2,128,128]{4,3,2,1,0:T(8,128)} custom-call(f32[8,1024,128]{2,1,0:T(8,128)S(1)} %get-tuple-element.8.gath_ref, f32[1024,128]{1,0:T(8,128)S(1)} %get-tuple-element.9.rest_ref, f32[1024,256]{1,0:T(8,128)S(1)} %get-tuple-element.10.weight_ref), custom_call_target="tpu_custom_call" | custom-call | tf_op jit(solution)/shard_map/pallas_call | solution.py:1380
Async XLA Ops:
  0.0 1.2 %copy-start = (f32[4,16,32,128]{3,2,1,0:T(8,128)S(1)}, f32[4,16,32,128]{3,2,1,0:T(8,128)}, u32[]{:S(2)}) copy-start(f32[4,16,32,128]{3,2,1,0:T(8,128)} %param.2) | copy-start | bytes 3145732
  1.2 0.8 copy-start.1
